TPU v7x, 32 devices: a whole 2x2x4 slice. The times are simulated.
32 devices in a mesh: grid: 2 (over y), wide: 8 (over z, x), band: 2 (over core).
Axes of the slice: x: 2, y: 2, z: 4, core: 2. Of those that a mesh axis runs over, the one named last changes fastest.
Arguments:
- energy: float32 [1152, 32, 256], P(None, ('grid', 'wide'), 'band'), parts along dimension 1, may hold values from -6 to 6
- source_weights: bfloat16 [2, 1152, 1152], P(None, 'band'), may hold values from -0.1875 to 0.1875
- speed: float32 [1152], replicated, may hold values from 0.15 to 0.9
- direction: int32 [1152], replicated, may hold values from 0 to 35
- sea_mask: int32 [32, 256], P('grid', 'band'), parts along dimension 0, may hold values 0 or 1
Outputs:
- forecast: float32 [1152, 32, 256], P(None, ('grid', 'wide'), 'band'), parts along dimension 1
There are 2 independent parts, one for each index of `grid`. A program takes and returns all parts, laid end to end along the dimension named above; an argument that names none is the same for every part. Nothing has to cross between parts.
Inputs may be any that keep to these rules, and one draw needn't show every extreme that they name: direction index of each bin, below 36.
All inputs are finite; a program needn't handle non-finite values. No bound on the sum of `sea_mask` on one device may be relied on, other than what follows from the above.
Results may differ from a plain program's by a relative error of at most 0.0011.
Values may be sent and summed in bfloat16 or wider, within the bound.
No kernel may reach another device: no remote copies, remote signals or barrier semaphores. Data moves between devices by JAX's collectives and lax.ppermute only.
A program may use at most 64 MiB of HBM per device.

v0:
```python
import math

import jax
import jax.numpy as jnp
from jax import lax
from jax.sharding import PartitionSpec as P

NDIR = 36


time_step = 0.5


def padded_2(cells, sides, width):
    for axis, dim in sides:
        count = lax.axis_size(axis)
        ends = count - 1
        head = lax.slice_in_dim(cells, 0, width, axis=dim)
        tail = lax.slice_in_dim(cells, cells.shape[dim] - width, cells.shape[dim], axis=dim)
        cells = jnp.concatenate(
            [
                lax.ppermute(tail, axis, [(i, (i + 1) % count) for i in range(ends)]),
                cells,
                lax.ppermute(head, axis, [((i + 1) % count, i) for i in range(ends)]),
            ],
            axis=dim,
        )
    return cells


def minmod_pair(first_value, second_value):
    return (
        0.5
        * (jnp.sign(first_value) + jnp.sign(second_value))
        * jnp.minimum(jnp.abs(first_value), jnp.abs(second_value))
    )


def take_cells(values, begin_at, how_many, sweep_axis):
    return lax.slice_in_dim(values, begin_at, begin_at + how_many, axis=sweep_axis)


def sweep(padded, courant, sweep_axis):
    cell_count = padded.shape[sweep_axis] - 4
    face_count = cell_count + 1
    cell_diffs = jnp.diff(padded, axis=sweep_axis)
    face_diff = take_cells(cell_diffs, 1, face_count, sweep_axis)
    behind = take_cells(cell_diffs, 0, face_count, sweep_axis)
    ahead_diff = take_cells(cell_diffs, 2, face_count, sweep_axis)
    left_cell = take_cells(padded, 1, face_count, sweep_axis)
    right_cell = take_cells(padded, 2, face_count, sweep_axis)
    forward = courant >= 0.0
    upwind = jnp.where(forward, left_cell, right_cell)
    limit_diff = jnp.where(forward, behind, ahead_diff)
    speed_abs = jnp.abs(courant)
    face_flux = courant * upwind + 0.5 * speed_abs * (1.0 - speed_abs) * minmod_pair(
        face_diff, limit_diff
    )
    centre = take_cells(padded, 2, cell_count, sweep_axis)
    return centre - (
        take_cells(face_flux, 1, cell_count, sweep_axis)
        - take_cells(face_flux, 0, cell_count, sweep_axis)
    )


def column_sweep(field_now, courant):
    padded = padded_2(field_now, (("band", 2),), 2)
    return sweep(padded, courant, 2)


def source_term(field_now, source_weights):
    bin_count = field_now.shape[0]
    point_count = field_now.shape[1] * field_now.shape[2]
    spectra = field_now.reshape(bin_count, point_count).astype(jnp.bfloat16)
    both_terms = jnp.einsum(
        "ikj,jp->ikp",
        lax.all_gather(source_weights, "band", axis=1, tiled=True),
        spectra,
        preferred_element_type=jnp.float32,
    )
    return (both_terms[0] * jax.nn.sigmoid(both_terms[1])).reshape(field_now.shape)


def local(energy, source_weights, speed, direction, sea_mask):
    row_dev = energy.shape[1]
    sea_cells = sea_mask.astype(jnp.float32)
    angle_all = (direction.astype(jnp.float32) + 0.5) * (2.0 * math.pi / NDIR)
    mask_here = lax.dynamic_slice_in_dim(sea_cells, lax.axis_index("wide") * row_dev, row_dev, 0)
    row_courant = (speed * jnp.sin(angle_all))[:, None, None]
    col_courant = (speed * jnp.cos(angle_all))[:, None, None]
    field_now = energy
    field_now = field_now + time_step * source_term(field_now, source_weights)
    padded = padded_2(field_now, (("wide", 1),), 2)
    field_now = sweep(padded, row_courant, 1)
    field_now = column_sweep(field_now, col_courant) * mask_here
    return field_now


def solution(mesh):
    return jax.shard_map(
        local,
        mesh=mesh,
        in_specs=(
            P(None, ("grid", "wide"), "band"),
            P(None, "band", None),
            P(),
            P(),
            P("grid", "band"),
        ),
        out_specs=P(None, ("grid", "wide"), "band"),
        check_vma=False,
    )
```

profile of v0, /device:TPU:9, one launch (start us, length us, event | category | flops | bytes accessed | tf_op | source)
XLA Modules:
  0.0 104.6 jit_solution(15222332604091012889)
XLA Ops:
  6.5 0.7 all-gather.2.cloned.1.call-update
  7.3 0.5 copy-done
  7.8 0.4 convert_element_type.12
  8.2 0.6 copy.9
  8.9 0.6 copy.12
  9.5 16.6 %all-gather.2.cloned.1.call-done = bf16[2,1152,1152]{2,1,0:T(8,128)(2,1)} async-done(((bf16[2,576,1152]{2,1,0:T(8,128)(2,1)}), bf16[2,1152,1152]{2,1,0:T(8,128)(2,1)}) %all-gather.2.cloned.1.call-update) | async-done | bytes 5308432 | tf_op jit(solution)/shard_map/all_gather | solution.py:77
  26.1 4.2 %fusion.15 = f32[2,1152,256]{1,2,0:T(8,128)S(1)} fusion(bf16[2,1152,1152]{2,1,0:T(8,128)(2,1)} %all-gather.2.cloned.1.call-done, bf16[1152,256,1]{0,1,2:T(8,128)(2,1)S(1)} %bitcast.7), kind=kOutput, calls=%fused_computation.36 | convolution fusion | flops 1358954496 | bytes 8257536 | tf_op jit(solution)/shard_map/ikj,jp->ikp/dot_general | solution.py:75
  30.3 0.3 fusion.13
  30.7 0.1 add.30
  30.8 3.1 %collective-permute-start = (f32[1152,2,128]{0,2,1:T(8,128)S(1)}, f32[1152,2,128]{0,2,1:T(8,128)S(1)}, u32[]{:S(2)}, u32[]{:S(2)}) collective-permute-start(f32[1152,2,128]{0,2,1:T(8,128)S(1)} %add.30), channel_id=1, source_target_pairs={{0,2},{2,4},{4,6},{6,8},{8,10},{10,12},{12,14},{1,3},{3,5},{5,7},{... | collective-permute-start | bytes 3538952 | tf_op jit(solution)/shard_map/ppermute | solution.py:22
  33.9 3.1 %collective-permute-start.1 = (f32[1152,2,128]{0,2,1:T(8,128)S(1)}, f32[1152,2,128]{0,2,1:T(8,128)S(1)}, u32[]{:S(2)}, u32[]{:S(2)}) collective-permute-start(f32[1152,2,128]{0,2,1:T(8,128)S(1)} %add.30), channel_id=1, source_target_pairs={{2,0},{4,2},{6,4},{8,6},{10,8},{12,10},{14,12},{3,1},{5,3},{7,5},{... | collective-permute-start | bytes 3538952 | tf_op jit(solution)/shard_map/ppermute | solution.py:24
  37.1 47.2 %collective-permute-done = f32[1152,2,128]{0,2,1:T(8,128)S(1)} collective-permute-done((f32[1152,2,128]{0,2,1:T(8,128)S(1)}, f32[1152,2,128]{0,2,1:T(8,128)S(1)}, u32[]{:S(2)}, u32[]{:S(2)}) %collective-permute-start) | collective-permute-done | bytes 1179680 | tf_op jit(solution)/shard_map/ppermute | solution.py:22
  84.3 2.5 %collective-permute-done.1 = f32[1152,2,128]{0,2,1:T(8,128)S(1)} collective-permute-done((f32[1152,2,128]{0,2,1:T(8,128)S(1)}, f32[1152,2,128]{0,2,1:T(8,128)S(1)}, u32[]{:S(2)}, u32[]{:S(2)}) %collective-permute-start.1) | collective-permute-done | bytes 1179680 | tf_op jit(solution)/shard_map/ppermute | solution.py:24
  86.8 0.2 pad_maximum_fusion
  87.0 0.2 slice_subtract_fusion
  87.3 1.4 %fusion.2 = f32[1152,3,128]{0,2,1:T(8,128)S(1)} fusion(f32[1152,2,128]{0,2,1:T(8,128)S(1)} %collective-permute-done.1, f32[1152,2,128]{0,2,1:T(8,128)S(1)} %add.30, f32[1152,2,128]{0,2,1:T(8,128)S(1)} %collective-permute-done, f32[1152,5,128]{0,2,1:T(8,128)S(1)} %slice_subtract_fusion, f32[1152]{0:T(1024)S(1)} %subtract_multiply_fusion.1, ...), kind=kLoop, calls=%fused_computation.6 | loop fusion | flops 6635520 | bytes 10627200 | tf_op jit(solution)/shard_map/add | solution.py:56
  88.7 0.1 fusion.8
  88.9 1.3 %collective-permute-start.2 = (f32[1152,2,2]{0,2,1:T(2,128)S(1)}, f32[1152,2,2]{0,2,1:T(2,128)S(1)}, u32[]{:S(2)}, u32[]{:S(2)}) collective-permute-start(f32[1152,2,2]{0,2,1:T(2,128)S(1)} %get-tuple-element.9), channel_id=1, source_target_pairs={{0,1},{2,3},{4,5},{6,7},{8,9},{10,11},{12,13},{14,15},{16,17},{18,... | collective-permute-start | bytes 55304 | tf_op jit(solution)/shard_map/ppermute | solution.py:22
  90.2 3.0 %collective-permute-start.3 = (f32[1152,2,2]{0,2,1:T(2,128)S(1)}, f32[1152,2,2]{0,2,1:T(2,128)S(1)}, u32[]{:S(2)}, u32[]{:S(2)}) collective-permute-start(f32[1152,2,2]{0,2,1:T(2,128)S(1)} %get-tuple-element.10), channel_id=1, source_target_pairs={{1,0},{3,2},{5,4},{7,6},{9,8},{11,10},{13,12},{15,14},{17,16},{19,... | collective-permute-start | bytes 55304 | tf_op jit(solution)/shard_map/ppermute | solution.py:24
  93.2 0.7 dynamic-slice_convert_fusion
  94.1 0.1 slice_subtract_fusion.1
  94.3 1.3 %fusion.5 = f32[1152,2,129]{0,2,1:T(8,128)S(1)} fusion(f32[1152,2,2]{0,2,1:T(2,128)S(1)} %collective-permute-done.3, f32[1152,2,128]{0,2,1:T(8,128)S(1)} %fusion.8, f32[1152,2,2]{0,2,1:T(2,128)S(1)} %collective-permute-done.2, f32[1152,2,131]{0,2,1:T(8,128)S(1)} %slice_subtract_fusion.1, f32[1152]{0:T(1024)S(1)} %subtract_multiply_fusion, ...), kind=kLoop, calls=%fused_computation.13 | loop fusion | flops 4458240 | bytes 5982336 | tf_op jit(solution)/shard_map/add | solution.py:56
  95.5 0.3 fusion.7
  95.8 1.9 %copy.10 = f32[1152,2,128]{2,1,0:T(2,128)} copy(f32[1152,2,128]{0,2,1:T(8,128)S(1)} %fusion.7) | data formatting | bytes 2359296 | tf_op jit(solution)/shard_map/mul | solution.py:95
  (13 shorter events, 0.3 us)
Async XLA Ops:
  6.5 1.3 %copy-start = (f32[1152,2,128]{2,1,0:T(2,128)S(1)}, f32[1152,2,128]{2,1,0:T(2,128)}, u32[]{:S(2)}) copy-start(f32[1152,2,128]{2,1,0:T(2,128)} %param.5) | copy-start | bytes 3538948
  6.5 19.6 %all-gather.2.cloned.1.call-start = ((), (), s32[]{:S(2)}) async-start(), calls=%async_computation | async-start | bytes 7962624 | tf_op jit(solution)/shard_map/all_gather | solution.py:77
  30.7 6.4 %copy-start.1 = (f32[1152]{0:T(1024)S(1)}, f32[1152]{0:T(1024)}, u32[]{:S(2)}) copy-start(f32[1152]{0:T(1024)} %param.7) | copy-start | bytes 13828
  30.7 6.4 %copy-start.2 = (s32[1152]{0:T(1024)S(1)}, s32[1152]{0:T(1024)}, u32[]{:S(2)}) copy-start(s32[1152]{0:T(1024)} %param.8) | copy-start | bytes 13828
  30.8 53.5 %collective-permute-start = (f32[1152,2,128]{0,2,1:T(8,128)S(1)}, f32[1152,2,128]{0,2,1:T(8,128)S(1)}, u32[]{:S(2)}, u32[]{:S(2)}) collective-permute-start(f32[1152,2,128]{0,2,1:T(8,128)S(1)} %add.30), channel_id=1, source_target_pairs={{0,2},{2,4},{4,6},{6,8},{8,10},{10,12},{12,14},{1,3},{3,5},{5,7},{... | collective-permute-start | bytes 3538952 | tf_op jit(solution)/shard_map/ppermute | solution.py:22
  33.9 52.9 %collective-permute-start.1 = (f32[1152,2,128]{0,2,1:T(8,128)S(1)}, f32[1152,2,128]{0,2,1:T(8,128)S(1)}, u32[]{:S(2)}, u32[]{:S(2)}) collective-permute-start(f32[1152,2,128]{0,2,1:T(8,128)S(1)} %add.30), channel_id=1, source_target_pairs={{2,0},{4,2},{6,4},{8,6},{10,8},{12,10},{14,12},{3,1},{5,3},{7,5},{... | collective-permute-start | bytes 3538952 | tf_op jit(solution)/shard_map/ppermute | solution.py:24
  88.9 5.0 %collective-permute-start.2 = (f32[1152,2,2]{0,2,1:T(2,128)S(1)}, f32[1152,2,2]{0,2,1:T(2,128)S(1)}, u32[]{:S(2)}, u32[]{:S(2)}) collective-permute-start(f32[1152,2,2]{0,2,1:T(2,128)S(1)} %get-tuple-element.9), channel_id=1, source_target_pairs={{0,1},{2,3},{4,5},{6,7},{8,9},{10,11},{12,13},{14,15},{16,17},{18,... | collective-permute-start | bytes 55304 | tf_op jit(solution)/shard_map/ppermute | solution.py:22
  90.2 3.9 %collective-permute-start.3 = (f32[1152,2,2]{0,2,1:T(2,128)S(1)}, f32[1152,2,2]{0,2,1:T(2,128)S(1)}, u32[]{:S(2)}, u32[]{:S(2)}) collective-permute-start(f32[1152,2,2]{0,2,1:T(2,128)S(1)} %get-tuple-element.10), channel_id=1, source_target_pairs={{1,0},{3,2},{5,4},{7,6},{9,8},{11,10},{13,12},{15,14},{17,16},{19,... | collective-permute-start | bytes 55304 | tf_op jit(solution)/shard_map/ppermute | solution.py:24
Sparse Core Ops, SparseCore 0:
  8.9 17.1 all-gather.1
where the time goes:
time: 105 us
  waiting for transfers between devices  67.1 us (64%)
  between operations  13.6 us (13%)
  starting transfers between devices  10.5 us (10%)
  other arithmetic  5.44 us (5%)
  matrix products  4.23 us (4%)
  local copies, waits for them, and re-layouts  3.76 us (4%)
    ppermute x2, waiting for transfers between devices, padded_2(): lax.ppermute(tail, axis, [(i, (i + 1) % count) for i in range(ends)])  47.2 us
    all_gather x1, waiting for transfers between devices, source_term(): lax.all_gather(source_weights, 'band', axis=1, tiled=True)  16.6 us
    ppermute x2, starting transfers between devices, padded_2(): lax.ppermute(head, axis, [((i + 1) % count, i) for i in range(ends)])  6.11 us
    ppermute x2, starting transfers between devices, padded_2(): lax.ppermute(tail, axis, [(i, (i + 1) % count) for i in range(ends)])  4.39 us
    dot_general x1, matrix products, source_term(): jnp.einsum('ikj,jp->ikp', lax.all_gather(source_weights, 'band', axis=1,...  4.23 us
    add x2, other arithmetic, sweep(): courant * upwind  2.71 us
    ppermute x2, waiting for transfers between devices, padded_2(): lax.ppermute(head, axis, [((i + 1) % count, i) for i in range(ends)])  2.61 us
  transfers between devices with their start and end apart: 5, of which 4 were waited for; matrix products, arithmetic and copies ran while one was open for 2% of the time, Pallas kernels for 0%

commit v1 on v0

v1 whole, which is shorter than its diff:
```python
import functools
import math

import jax
import jax.numpy as jnp
from jax import lax
from jax.experimental import pallas as pl
from jax.experimental.pallas import tpu as pltpu
from jax.sharding import PartitionSpec as P

NDIR = 36
TIME_STEP = 0.5
CHUNKS = 3
GROUPS = 8
F32 = jnp.float32
BF16 = jnp.bfloat16
VMEM = pl.BlockSpec(memory_space=pltpu.VMEM)
SMEM = pl.BlockSpec(memory_space=pltpu.SMEM)
HBM = pl.BlockSpec(memory_space=pltpu.HBM)
ANY = pl.BlockSpec(memory_space=pl.ANY)


def call(kernel, mib, **kw):
    return pl.pallas_call(
        kernel,
        compiler_params=pltpu.CompilerParams(vmem_limit_bytes=mib * 1024 * 1024), **kw,
    )


def in_hbm(x):
    return pltpu.with_memory_space_constraint(x, pltpu.HBM)


def chunk_sizes(bins):
    tiles = bins // 128
    cuts = [tiles * i // CHUNKS for i in range(CHUNKS + 1)]
    return [(b - a) * 128 for a, b in zip(cuts, cuts[1:]) if b > a]


def prepare_kernel(energy, *refs):
    *parts, held, sems = refs
    piece = 128
    copies = []
    for i in range(held.shape[0] // (2 * piece)):
        at = pl.ds(2 * i * piece, 2 * piece)
        copies.append(pltpu.make_async_copy(energy.at[at, :], held.at[at, :], sems.at[i]))
        copies[-1].start()
    i = 0
    for part in parts:
        for k in range(0, part.shape[1], piece):
            copies[i].wait()
            for row in range(2):
                part[row, k : k + piece, :] = held[pl.ds(2 * i * piece + row, piece, stride=2), :].astype(BF16)
            i += 1


def gather_points(parts, points, start=0):
    for part in parts:
        size = part.shape[1]
        for row in range(2):
            points[pl.ds(start, size), row * 128 : (row + 1) * 128] = part[row]
        start += size


def blocks(band, mine, other, bins):
    size = bins // GROUPS
    half = mine.shape[1]
    for weights, start in ((mine, band * half), (other, (1 - band) * half)):
        for k in range(0, half, size):
            yield weights, slice(k, k + size), pl.multiple_of(start + k, 16)


def dots(weights, rows, points, first=0):
    part = slice(first, first + points.shape[0])
    return [jnp.dot(weights[i, rows, part], points[...], preferred_element_type=F32) for i in range(2)]


def gained(grow, gate):
    return TIME_STEP * (grow * jax.nn.sigmoid(gate))


def row_cells(row):
    return slice(row * 128, (row + 1) * 128)


def own_kernel(band_ref, mine, other, energy, courants, *refs):
    *parts, field, other_here, points, held, sems = refs
    bins = points.shape[0]
    size = bins // GROUPS
    copies = []
    for j, k in enumerate(range(0, mine.shape[1], size)):
        rows = pl.ds(k, size)
        copies.append(pltpu.make_async_copy(other.at[:, rows, :], other_here.at[:, rows, :], sems.at[j]))
    energy_copy = pltpu.make_async_copy(energy, held, sems.at[len(copies)])
    energy_copy.start()
    for copy in copies:
        copy.start()
    gather_points(parts, points)
    for n, (weights, rows, at) in enumerate(blocks(band_ref[0], mine, other_here, bins)):
        if n >= len(copies):
            copies[n - len(copies)].wait()
        src = gained(*dots(weights, rows, points))
        if n == 0:
            energy_copy.wait()
        for row in range(2):
            field[row, pl.ds(at, size), :] = held[pl.ds(2 * at + row, size, stride=2), :] + src[:, row_cells(row)]


def near_kernel(band_ref, mine, other, *refs):
    *parts, field, points = refs
    bins = points.shape[0]
    size = bins // GROUPS
    gather_points(parts, points)
    for weights, rows, at in blocks(band_ref[0], mine, other, bins):
        src = gained(*dots(weights, rows, points))
        for row in range(2):
            field[row, pl.ds(at, size), :] = points[pl.ds(at, size), row_cells(row)].astype(F32) + src[:, row_cells(row)]


def inside_points(wide_ref, last, parts, points, start=0):
    w = wide_ref[0]
    inside = (w != 0) & (w != last)

    @pl.when(inside)
    def _():
        gather_points(parts, points, start)

    @pl.when(jnp.logical_not(inside))
    def _():
        size = sum(part.shape[1] for part in parts)
        points[pl.ds(start, size), :] = jnp.zeros((size, points.shape[1]), points.dtype)


def partial_kernel(last, band_ref, wide_ref, mine, other, *refs):
    *parts, sums, points = refs
    bins = sums.shape[1]
    inside_points(wide_ref, last, parts, points)
    for weights, rows, at in blocks(band_ref[0], mine, other, bins):
        for i, value in enumerate(dots(weights, rows, points)):
            sums[i, pl.ds(at, value.shape[0]), :] = value


def limited(a, b):
    return jnp.minimum(jnp.maximum(a, jnp.minimum(b, 0.0)), jnp.maximum(b, 0.0))


def row_kernel(last, band_ref, wide_ref, mine, other, sums, courants, own, near, *refs):
    *parts, field, edge, points, far = refs
    bins = points.shape[0]
    first = bins - parts[-1].shape[1]
    size = bins // GROUPS
    band, odd = band_ref[0], lax.rem(wide_ref[0], 2)
    inside_points(wide_ref, last, parts, points)
    late = points.at[first:, :]
    shift = jnp.where(band == 0, 1, 127)
    lane = lax.broadcasted_iota(jnp.int32, (8, 128), 1)

    def sweep(weights, rows, at, behind, ahead, group, begin):
        mark = (lane - 2 * group) & 127
        mark0 = (mark == 0) | (mark == 127)
        mark1 = (mark == 64) | (mark == 63)
        shift0 = (shift + 2 * group) & 127
        shift1 = (shift0 + 64) & 127
        grow, gate = dots(weights, rows, late, first)
        src = gained(sums[0, pl.ds(at, size), :] + grow, sums[1, pl.ds(at, size), :] + gate)
        for row in range(2):
            base = points[pl.ds(at, size), row_cells(row)].astype(F32)
            far[row, pl.ds(at, size), :] = base + src[:, row_cells(row)]
        for i in range(0, size, 8):
            here = pl.ds(pl.multiple_of(at + i, 8), 8)
            c, k = courants[0, here, :], courants[1, here, :]
            forward = c >= 0.0
            a = jnp.abs(c)
            q0, q1 = own[0, here, :], own[1, here, :]
            m2 = jnp.where(forward, behind[0, here, :], ahead[1, here, :])
            m1 = jnp.where(forward, behind[1, here, :], ahead[0, here, :])
            c0 = jnp.where(forward, q0, q1)
            c1 = jnp.where(forward, q1, q0)
            p2 = jnp.where(forward, ahead[0, here, :], behind[1, here, :])
            da, db, dc, dd = m1 - m2, c0 - m1, c1 - c0, p2 - c1
            fa = a * m1 + k * limited(db, da)
            fb = a * c0 + k * limited(dc, db)
            fc = a * c1 + k * limited(dd, dc)
            n0 = c0 - (fb - fa)
            n1 = c1 - (fc - fb)
            o0 = jnp.where(forward, n0, n1)
            o1 = jnp.where(forward, n1, n0)
            field[0, here, :] = o0
            field[1, here, :] = o1
            before = jnp.zeros_like(o0) if begin else edge[i : i + 8, :]
            before = jnp.where(mark1, pltpu.roll(o1, shift1, axis=1), before)
            edge[i : i + 8, :] = jnp.where(mark0, pltpu.roll(o0, shift0, axis=1), before)

    def run(behind, ahead):
        for n, (weights, rows, at) in enumerate(blocks(band, mine, other, bins)):
            group = lax.rem(band * (GROUPS // 2) + n, GROUPS)
            sweep(weights, rows, at, behind, ahead, group, n == 0)

    @pl.when(odd == 1)
    def _():
        run(near, far)

    @pl.when(odd == 0)
    def _():
        run(far, near)


def col_kernel(band_ref, wide_ref, courants, sea, field, beside, out, held, sems):
    lane = lax.broadcasted_iota(jnp.int32, (8, 128), 1)
    first, last = lane == 0, lane == 127
    outer = first | last
    band = band_ref[0]
    left = band.astype(F32)
    right = 1.0 - left
    sign = right - left
    shift = jnp.where(band == 1, 1, 127)
    bins = courants.shape[1]
    size = bins // GROUPS
    place = 2 * wide_ref[0]
    mask = [jnp.broadcast_to(sea[pl.ds(place + row, 1), :].astype(F32), (8, 128)) for row in range(2)]
    shared = jnp.where(first, left, right) > 0.5

    def body(i, carry):
        i = pl.multiple_of(i * 8, 8)
        folded = beside[pl.ds(i, 8), :]
        for group in range(GROUPS):
            at = pl.multiple_of(group * size + i, 8)
            here = pl.ds(at, 8)
            c, k = courants[2, here, :], courants[3, here, :]
            forward = c >= 0.0
            a = jnp.abs(c)
            h1 = pltpu.roll(folded, (128 - 2 * group) & 127, axis=1) if group else folded
            h2 = pltpu.roll(folded, (shift + 128 - 2 * group) & 127, axis=1)
            q0, q1 = field[0, here, :], field[1, here, :]
            ends = jnp.where(outer, q0, pltpu.roll(q1, 64, axis=1))
            ge = a * h1 + (sign * k) * limited(h1 - ends, h2 - h1)
            ends_at = (first & forward) | (last & jnp.logical_not(forward))
            for row, q in ((0, q0), (1, q1)):
                h, e = (h1, ge) if row == 0 else (pltpu.roll(h1, 64, axis=1), pltpu.roll(ge, 64, axis=1))
                h = jnp.where(shared, h, 0.0)
                e = jnp.where(shared, e, 0.0)
                d = jnp.where(last, h, pltpu.roll(q, 127, axis=1)) - q
                dm = jnp.where(first, q - h, pltpu.roll(d, 1, axis=1))
                g = a * q + k * limited(d, dm)
                t = jnp.where(forward, pltpu.roll(g, 1, axis=1), pltpu.roll(g, 127, axis=1))
                t = jnp.where(ends_at, e, t)
                held[pl.ds(2 * at + row, 8, stride=2), :] = (q - (g - t)) * mask[row]
        return carry

    copies = []
    step = size // 3
    for part in range(3):
        lax.fori_loop(part * step // 8, (part + 1) * step // 8, body, 0)
        for group in range(GROUPS):
            rows = pl.ds(2 * (group * size + part * step), 2 * step)
            copies.append(pltpu.make_async_copy(held.at[rows, :], out.at[rows, :], sems.at[len(copies)]))
            copies[-1].start()
    for copy in copies:
        copy.wait()


def ring(count):
    order = list(range(0, count, 2)) + list(range(count - 1, 0, -2))
    return list(zip(order, order[1:] + order[:1]))


def local(energy, source_weights, speed, direction, sea_mask):
    bins, rows, cols = energy.shape
    wide, bands = lax.axis_size("wide"), lax.axis_size("band")
    if rows != 2 or cols != 128 or wide % 2 or bands != 2 or bins % (48 * GROUPS):
        raise ValueError("block shape")
    w_at = lax.axis_index("wide").astype(jnp.int32).reshape(1)
    b_at = lax.axis_index("band").astype(jnp.int32).reshape(1)
    flat = energy.reshape(bins * rows, cols)
    sizes = chunk_sizes(bins)
    swap = [(i, i ^ 1) for i in range(wide)]
    beside = [(i, i ^ 1) for i in range(bands)]

    other = lax.ppermute(source_weights, "band", beside)
    parts = call(
        prepare_kernel, 8,
        out_shape=[jax.ShapeDtypeStruct((2, n, cols), BF16) for n in sizes],
        in_specs=[HBM], out_specs=[VMEM] * len(sizes),
        scratch_shapes=[pltpu.VMEM((2 * bins, cols), F32), pltpu.SemaphoreType.DMA((bins // 128,))],
    )(in_hbm(flat))
    swapped, relayed = [], []
    for part in parts:
        swapped.append(lax.ppermute(part, "wide", swap))
    for part in swapped:
        relayed.append(lax.ppermute(part, "wide", ring(wide)))

    angle = (direction.astype(F32) + 0.5) * (2.0 * math.pi / NDIR)
    row_c, col_c = speed * jnp.sin(angle), speed * jnp.cos(angle)
    row_k, col_k = [0.5 * jnp.abs(c) * (1.0 - jnp.abs(c)) for c in (row_c, col_c)]
    table = jnp.stack([row_c, row_k, col_c, jnp.where(col_c >= 0.0, col_k, -col_k)])
    courants = jnp.broadcast_to(table[:, :, None], (4, bins, cols))

    full = jax.ShapeDtypeStruct((2, bins, cols), F32)
    sums = jax.ShapeDtypeStruct((2, bins, 2 * cols), F32)
    points = pltpu.VMEM((bins, 2 * cols), BF16)
    n = len(sizes)
    own, other = call(
        own_kernel, 8,
        out_shape=[full, jax.ShapeDtypeStruct(source_weights.shape, BF16)],
        in_specs=[SMEM, VMEM, HBM, HBM, ANY] + [VMEM] * n, out_specs=[VMEM, VMEM],
        scratch_shapes=[points, pltpu.VMEM((2 * bins, cols), F32), pltpu.SemaphoreType.DMA((GROUPS // 2 + 1,))],
    )(b_at, source_weights, in_hbm(other), in_hbm(flat), courants, *parts)
    near = call(
        near_kernel, 8, out_shape=full, in_specs=[SMEM] + [VMEM] * (2 + n),
        out_specs=VMEM, scratch_shapes=[points],
    )(b_at, source_weights, other, *swapped)
    early = call(
        functools.partial(partial_kernel, wide - 1), 8, out_shape=sums,
        in_specs=[SMEM, SMEM] + [VMEM] * (1 + n), out_specs=VMEM,
        scratch_shapes=[pltpu.VMEM((bins - sizes[-1], 2 * cols), BF16)],
    )(b_at, w_at, source_weights, other, *relayed[:-1])
    field, edge = call(
        functools.partial(row_kernel, wide - 1), 10,
        out_shape=[full, jax.ShapeDtypeStruct((bins // GROUPS, cols), F32)],
        in_specs=[SMEM, SMEM] + [VMEM] * (6 + n), out_specs=[VMEM, VMEM],
        scratch_shapes=[points, pltpu.VMEM((2, bins, cols), F32)],
    )(b_at, w_at, source_weights, other, early, courants, own, near, *relayed)
    edges = lax.ppermute(edge, "band", beside)
    out = call(
        col_kernel, 10, out_shape=jax.ShapeDtypeStruct((bins * rows, cols), F32),
        in_specs=[SMEM, SMEM] + [VMEM] * 4, out_specs=HBM,
        scratch_shapes=[pltpu.VMEM((bins * rows, cols), F32), pltpu.SemaphoreType.DMA((3 * GROUPS,))],
    )(b_at, w_at, courants, sea_mask, field, edges)
    return out.reshape(bins, rows, cols)


def solution(mesh):
    return jax.shard_map(
        local,
        mesh=mesh,
        in_specs=(
            P(None, ("grid", "wide"), "band"),
            P(None, "band", None),
            P(),
            P(),
            P("grid", "band"),
        ),
        out_specs=P(None, ("grid", "wide"), "band"),
        check_vma=False,
    )
```

time: 105 us -> 41.8 us (0.40)
  the two profiles are of different devices: /device:TPU:9 before, /device:TPU:0 now
where the time goes in v1:
time: 41.8 us; the launch traced here: 41.6 us
  Pallas kernels  18.4 us (44%)
  starting transfers between devices  10.9 us (26%)
  waiting for transfers between devices  10.7 us (26%)
  other arithmetic  0.79 us (2%)
  local copies, waits for them, and re-layouts  0.69 us (2%)
    ppermute x3, waiting for transfers between devices, local(): swapped.append(lax.ppermute(part, 'wide', swap))  7.11 us
    pallas_call x1, Pallas kernels, local(): call(col_kernel, 10, out_shape=jax.ShapeDtypeStruct((bins * rows, cols),...  6.77 us
    ppermute x3, starting transfers between devices, local(): relayed.append(lax.ppermute(part, 'wide', ring(wide)))  5.83 us
    pallas_call x1, Pallas kernels, local(): call(own_kernel, 8, out_shape=[full, jax.ShapeDtypeStruct(source_weights....  4.83 us
    ppermute x3, starting transfers between devices, local(): swapped.append(lax.ppermute(part, 'wide', swap))  4.48 us
    pallas_call x1, Pallas kernels, local(): call(prepare_kernel, 8, out_shape=[jax.ShapeDtypeStruct((2, n, cols), BF1...  2.38 us
    ppermute x3, waiting for transfers between devices, local(): relayed.append(lax.ppermute(part, 'wide', ring(wide)))  2.37 us
    pallas_call x1, Pallas kernels, local(): call(near_kernel, 8, out_shape=full, in_specs=[SMEM] + [VMEM] * (2 + n),...  1.74 us
  transfers between devices with their start and end apart: 8, of which 5 were waited for; matrix products, arithmetic and copies ran while one was open for 4% of the time, Pallas kernels for 24%

profile of v1, /device:TPU:0, one launch (start us, length us, event | category | flops | bytes accessed | tf_op | source)
XLA Modules:
  0.0 41.6 jit_solution(2185014468828970424)
XLA Ops:
  0.0 0.5 %collective-permute-start = (bf16[2,576,1152]{2,1,0:T(8,128)(2,1)}, bf16[2,576,1152]{2,1,0:T(8,128)(2,1)}, u32[]{:S(2)}, u32[]{:S(2)}) collective-permute-start(bf16[2,576,1152]{2,1,0:T(8,128)(2,1)} %mine.7), channel_id=1, source_target_pairs={{0,1},{1,0},{2,3},{3,2},{4,5},{5,4},{6,7},{7,6},{8,9},{9,8},{10,11... | collective-permute-start | bytes 7962632 | tf_op jit(solution)/shard_map/ppermute | solution.py:279
  0.5 2.4 %shard_map.55 = (bf16[2,384,128]{2,1,0:T(8,128)(2,1)S(1)}, bf16[2,384,128]{2,1,0:T(8,128)(2,1)}, bf16[2,384,128]{2,1,0:T(8,128)(2,1)}) custom-call(f32[2304,128]{1,0:T(8,128)} %bitcast.4), custom_call_target="tpu_custom_call" | custom-call | tf_op jit(solution)/shard_map/pallas_call | solution.py:280
  2.9 2.4 %collective-permute-start.1 = (bf16[2,384,128]{2,1,0:T(8,128)(2,1)S(1)}, bf16[2,384,128]{2,1,0:T(8,128)(2,1)S(1)}, u32[]{:S(2)}, u32[]{:S(2)}) collective-permute-start(bf16[2,384,128]{2,1,0:T(8,128)(2,1)S(1)} %get-tuple-element.12.refs_0_), channel_id=1, source_target_pairs={{0,2},{2,0},{4,6},{6,4},{8,10},{10,8},{12,14},{14,12},{1,3},{3,1},... | collective-permute-start | bytes 589832 | tf_op jit(solution)/shard_map/ppermute | solution.py:288
  5.3 0.1 collective-permute-start.3
  5.4 1.9 %collective-permute-start.5 = (bf16[2,384,128]{2,1,0:T(8,128)(2,1)}, bf16[2,384,128]{2,1,0:T(8,128)(2,1)S(1)}, u32[]{:S(2)}, u32[]{:S(2)}) collective-permute-start(bf16[2,384,128]{2,1,0:T(8,128)(2,1)} %get-tuple-element.14.refs_2_), channel_id=1, source_target_pairs={{0,2},{2,0},{4,6},{6,4},{8,10},{10,8},{12,14},{14,12},{1,3},{3,1},... | collective-permute-start | bytes 589832 | tf_op jit(solution)/shard_map/ppermute | solution.py:288
  7.4 0.8 %subtract_multiply_fusion = (f32[1152]{0:T(1024)S(1)}, f32[1152]{0:T(1024)S(1)}, f32[1152]{0:T(1024)S(1)}, f32[1152]{0:T(1024)S(1)}) fusion(f32[1152]{0:T(1024)} %param.7, s32[1152]{0:T(1024)} %param.8), kind=kLoop, calls=%fused_computation.3 | loop fusion | flops 18432 | bytes 27648 | tf_op jit(solution)/shard_map/mul | solution.py:294
  8.2 2.9 %collective-permute-done.1.refs_0_ = bf16[2,384,128]{2,1,0:T(8,128)(2,1)S(1)} collective-permute-done((bf16[2,384,128]{2,1,0:T(8,128)(2,1)S(1)}, bf16[2,384,128]{2,1,0:T(8,128)(2,1)S(1)}, u32[]{:S(2)}, u32[]{:S(2)}) %collective-permute-start.1) | collective-permute-done | bytes 196640 | tf_op jit(solution)/shard_map/ppermute | solution.py:288
  11.1 2.1 %collective-permute-start.2 = (bf16[2,384,128]{2,1,0:T(8,128)(2,1)S(1)}, bf16[2,384,128]{2,1,0:T(8,128)(2,1)S(1)}, u32[]{:S(2)}, u32[]{:S(2)}) collective-permute-start(bf16[2,384,128]{2,1,0:T(8,128)(2,1)S(1)} %collective-permute-done.1.refs_0_), channel_id=1, source_target_pairs={{0,4},{4,8},{8,12},{12,14},{14,10},{10,6},{6,2},{2,0},{1,5},{5,9},... | collective-permute-start | bytes 589832 | tf_op jit(solution)/shard_map/ppermute | solution.py:290
  13.2 2.1 %collective-permute-done.3.refs_1_ = bf16[2,384,128]{2,1,0:T(8,128)(2,1)S(1)} collective-permute-done((bf16[2,384,128]{2,1,0:T(8,128)(2,1)}, bf16[2,384,128]{2,1,0:T(8,128)(2,1)S(1)}, u32[]{:S(2)}, u32[]{:S(2)}) %collective-permute-start.3) | collective-permute-done | bytes 196640 | tf_op jit(solution)/shard_map/ppermute | solution.py:288
  15.3 2.1 %collective-permute-start.4 = (bf16[2,384,128]{2,1,0:T(8,128)(2,1)S(1)}, bf16[2,384,128]{2,1,0:T(8,128)(2,1)S(1)}, u32[]{:S(2)}, u32[]{:S(2)}) collective-permute-start(bf16[2,384,128]{2,1,0:T(8,128)(2,1)S(1)} %collective-permute-done.3.refs_1_), channel_id=1, source_target_pairs={{0,4},{4,8},{8,12},{12,14},{14,10},{10,6},{6,2},{2,0},{1,5},{5,9},... | collective-permute-start | bytes 589832 | tf_op jit(solution)/shard_map/ppermute | solution.py:290
  17.4 2.1 %collective-permute-done.5.refs_2_ = bf16[2,384,128]{2,1,0:T(8,128)(2,1)S(1)} collective-permute-done((bf16[2,384,128]{2,1,0:T(8,128)(2,1)}, bf16[2,384,128]{2,1,0:T(8,128)(2,1)S(1)}, u32[]{:S(2)}, u32[]{:S(2)}) %collective-permute-start.5) | collective-permute-done | bytes 196640 | tf_op jit(solution)/shard_map/ppermute | solution.py:288
  19.5 1.6 %collective-permute-start.6 = (bf16[2,384,128]{2,1,0:T(8,128)(2,1)S(1)}, bf16[2,384,128]{2,1,0:T(8,128)(2,1)S(1)}, u32[]{:S(2)}, u32[]{:S(2)}) collective-permute-start(bf16[2,384,128]{2,1,0:T(8,128)(2,1)S(1)} %collective-permute-done.5.refs_2_), channel_id=1, source_target_pairs={{0,4},{4,8},{8,12},{12,14},{14,10},{10,6},{6,2},{2,0},{1,5},{5,9},... | collective-permute-start | bytes 589832 | tf_op jit(solution)/shard_map/ppermute | solution.py:290
  21.2 0.0 collective-permute-done.other
  21.2 0.7 %broadcast_in_dim.2.courants = f32[4,1152,128]{2,1,0:T(8,128)S(1)} broadcast(f32[4,1152]{1,0:T(4,128)S(1)} %pad_maximum_fusion), dimensions={0,1} | broadcast | bytes 2377728 | tf_op jit(solution)/shard_map/broadcast_in_dim | solution.py:296
  21.8 4.8 %shard_map.56 = (f32[2,1152,128]{2,1,0:T(8,128)S(1)}, bf16[2,576,1152]{2,1,0:T(8,128)(2,1)S(1)}) custom-call(s32[1]{0:T(128)} %bitcast.band_ref, bf16[2,576,1152]{2,1,0:T(8,128)(2,1)S(1)} %copy-done, bf16[2,576,1152]{2,1,0:T(8,128)(2,1)} %collective-permute-done.other, f32[2304,128]{1,0:T(8,128)} %bitcast.5, f32[4,1152,128]{2,1,0:T(8,128)S(1)} %broadcast_in_dim.2.courants, ...), custom_call_target="tpu_custom_call" | custom-call | tf_op jit(solution)/shard_map/pallas_call | solution.py:302
  26.7 1.7 %shard_map.58.near = f32[2,1152,128]{2,1,0:T(8,128)S(1)} custom-call(s32[1]{0:T(128)} %bitcast.band_ref, bf16[2,576,1152]{2,1,0:T(8,128)(2,1)S(1)} %copy-done, bf16[2,576,1152]{2,1,0:T(8,128)(2,1)S(1)} %get-tuple-element.15.other, bf16[2,384,128]{2,1,0:T(8,128)(2,1)S(1)} %collective-permute-done.1.refs_0_, ...), custom_call_target="tpu_custom_call" | custom-call | tf_op jit(solution)/shard_map/pallas_call | solution.py:308
  28.4 0.0 collective-permute-done.2.refs_0_
  28.4 0.0 collective-permute-done.4.refs_1_
  28.4 1.1 %shard_map.57.sums = f32[2,1152,256]{2,1,0:T(8,128)S(1)} custom-call(s32[1]{0:T(128)} %bitcast.band_ref, s32[1]{0:T(128)} %bitcast.1.wide_ref, bf16[2,576,1152]{2,1,0:T(8,128)(2,1)S(1)} %copy-done, bf16[2,576,1152]{2,1,0:T(8,128)(2,1)S(1)} %get-tuple-element.15.other, bf16[2,384,128]{2,1,0:T(8,128)(2,1)S(1)} %collective-permute-done.2.refs_0_, ...), custom_call_target="tpu_custom_call" | custom-call | tf_op jit(solution)/shard_map/pallas_call | solution.py:312
  29.6 2.4 %collective-permute-done.6.refs_2_ = bf16[2,384,128]{2,1,0:T(8,128)(2,1)S(1)} collective-permute-done((bf16[2,384,128]{2,1,0:T(8,128)(2,1)S(1)}, bf16[2,384,128]{2,1,0:T(8,128)(2,1)S(1)}, u32[]{:S(2)}, u32[]{:S(2)}) %collective-permute-start.6) | collective-permute-done | bytes 196640 | tf_op jit(solution)/shard_map/ppermute | solution.py:290
  31.9 1.5 %shard_map.59 = (f32[2,1152,128]{2,1,0:T(8,128)S(1)}, f32[144,128]{1,0:T(8,128)S(1)}) custom-call(s32[1]{0:T(128)} %bitcast.band_ref, s32[1]{0:T(128)} %bitcast.1.wide_ref, bf16[2,576,1152]{2,1,0:T(8,128)(2,1)S(1)} %copy-done, bf16[2,576,1152]{2,1,0:T(8,128)(2,1)S(1)} %get-tuple-element.15.other, f32[2,1152,256]{2,1,0:T(8,128)S(1)} %shard_map.57.sums, ...), custom_call_target="tpu_custom_call" | custom-call | tf_op jit(solution)/shard_map/pallas_call | solution.py:317
  33.5 0.1 collective-permute-start.7
  33.5 1.3 %collective-permute-done.7.beside = f32[144,128]{1,0:T(8,128)S(1)} collective-permute-done((f32[144,128]{1,0:T(8,128)S(1)}, f32[144,128]{1,0:T(8,128)S(1)}, u32[]{:S(2)}, u32[]{:S(2)}) %collective-permute-start.7) | collective-permute-done | bytes 73760 | tf_op jit(solution)/shard_map/ppermute | solution.py:323
  34.8 6.8 %shard_map.60 = f32[2304,128]{1,0:T(8,128)} custom-call(s32[1]{0:T(128)} %bitcast.band_ref, s32[1]{0:T(128)} %bitcast.1.wide_ref, f32[4,1152,128]{2,1,0:T(8,128)S(1)} %broadcast_in_dim.2.courants, s32[16,128]{1,0:T(8,128)S(1)} %copy-done.1, f32[2,1152,128]{2,1,0:T(8,128)S(1)} %get-tuple-element.17.field, f32[144,128]{1,0:T(8,128)S(1)} %collective-permute-done.7.beside), custom_call_target="tpu_custom_call" | custom-call | tf_op jit(solution)/shard_map/pallas_call | solution.py:324
  (9 shorter events, 0.1 us)
Async XLA Ops:
  0.0 21.8 %copy-start = (bf16[2,576,1152]{2,1,0:T(8,128)(2,1)S(1)}, bf16[2,576,1152]{2,1,0:T(8,128)(2,1)}, u32[]{:S(2)}) copy-start(bf16[2,576,1152]{2,1,0:T(8,128)(2,1)} %mine.7) | copy-start | bytes 7962628
  0.0 21.2 %collective-permute-start = (bf16[2,576,1152]{2,1,0:T(8,128)(2,1)}, bf16[2,576,1152]{2,1,0:T(8,128)(2,1)}, u32[]{:S(2)}, u32[]{:S(2)}) collective-permute-start(bf16[2,576,1152]{2,1,0:T(8,128)(2,1)} %mine.7), channel_id=1, source_target_pairs={{0,1},{1,0},{2,3},{3,2},{4,5},{5,4},{6,7},{7,6},{8,9},{9,8},{10,11... | collective-permute-start | bytes 7962632 | tf_op jit(solution)/shard_map/ppermute | solution.py:279
  2.9 8.2 %collective-permute-start.1 = (bf16[2,384,128]{2,1,0:T(8,128)(2,1)S(1)}, bf16[2,384,128]{2,1,0:T(8,128)(2,1)S(1)}, u32[]{:S(2)}, u32[]{:S(2)}) collective-permute-start(bf16[2,384,128]{2,1,0:T(8,128)(2,1)S(1)} %get-tuple-element.12.refs_0_), channel_id=1, source_target_pairs={{0,2},{2,0},{4,6},{6,4},{8,10},{10,8},{12,14},{14,12},{1,3},{3,1},... | collective-permute-start | bytes 589832 | tf_op jit(solution)/shard_map/ppermute | solution.py:288
  5.3 10.0 %collective-permute-start.3 = (bf16[2,384,128]{2,1,0:T(8,128)(2,1)}, bf16[2,384,128]{2,1,0:T(8,128)(2,1)S(1)}, u32[]{:S(2)}, u32[]{:S(2)}) collective-permute-start(bf16[2,384,128]{2,1,0:T(8,128)(2,1)} %get-tuple-element.13.refs_1_), channel_id=1, source_target_pairs={{0,2},{2,0},{4,6},{6,4},{8,10},{10,8},{12,14},{14,12},{1,3},{3,1},... | collective-permute-start | bytes 589832 | tf_op jit(solution)/shard_map/ppermute | solution.py:288
  5.4 14.1 %collective-permute-start.5 = (bf16[2,384,128]{2,1,0:T(8,128)(2,1)}, bf16[2,384,128]{2,1,0:T(8,128)(2,1)S(1)}, u32[]{:S(2)}, u32[]{:S(2)}) collective-permute-start(bf16[2,384,128]{2,1,0:T(8,128)(2,1)} %get-tuple-element.14.refs_2_), channel_id=1, source_target_pairs={{0,2},{2,0},{4,6},{6,4},{8,10},{10,8},{12,14},{14,12},{1,3},{3,1},... | collective-permute-start | bytes 589832 | tf_op jit(solution)/shard_map/ppermute | solution.py:288
  11.1 17.3 %collective-permute-start.2 = (bf16[2,384,128]{2,1,0:T(8,128)(2,1)S(1)}, bf16[2,384,128]{2,1,0:T(8,128)(2,1)S(1)}, u32[]{:S(2)}, u32[]{:S(2)}) collective-permute-start(bf16[2,384,128]{2,1,0:T(8,128)(2,1)S(1)} %collective-permute-done.1.refs_0_), channel_id=1, source_target_pairs={{0,4},{4,8},{8,12},{12,14},{14,10},{10,6},{6,2},{2,0},{1,5},{5,9},... | collective-permute-start | bytes 589832 | tf_op jit(solution)/shard_map/ppermute | solution.py:290
  15.3 13.1 %collective-permute-start.4 = (bf16[2,384,128]{2,1,0:T(8,128)(2,1)S(1)}, bf16[2,384,128]{2,1,0:T(8,128)(2,1)S(1)}, u32[]{:S(2)}, u32[]{:S(2)}) collective-permute-start(bf16[2,384,128]{2,1,0:T(8,128)(2,1)S(1)} %collective-permute-done.3.refs_1_), channel_id=1, source_target_pairs={{0,4},{4,8},{8,12},{12,14},{14,10},{10,6},{6,2},{2,0},{1,5},{5,9},... | collective-permute-start | bytes 589832 | tf_op jit(solution)/shard_map/ppermute | solution.py:290
  19.5 12.4 %collective-permute-start.6 = (bf16[2,384,128]{2,1,0:T(8,128)(2,1)S(1)}, bf16[2,384,128]{2,1,0:T(8,128)(2,1)S(1)}, u32[]{:S(2)}, u32[]{:S(2)}) collective-permute-start(bf16[2,384,128]{2,1,0:T(8,128)(2,1)S(1)} %collective-permute-done.5.refs_2_), channel_id=1, source_target_pairs={{0,4},{4,8},{8,12},{12,14},{14,10},{10,6},{6,2},{2,0},{1,5},{5,9},... | collective-permute-start | bytes 589832 | tf_op jit(solution)/shard_map/ppermute | solution.py:290
  31.9 2.9 %copy-start.1 = (s32[16,128]{1,0:T(8,128)S(1)}, s32[16,128]{1,0:T(8,128)}, u32[]{:S(2)}) copy-start(s32[16,128]{1,0:T(8,128)} %sea.1) | copy-start | bytes 24580
  33.5 1.3 %collective-permute-start.7 = (f32[144,128]{1,0:T(8,128)S(1)}, f32[144,128]{1,0:T(8,128)S(1)}, u32[]{:S(2)}, u32[]{:S(2)}) collective-permute-start(f32[144,128]{1,0:T(8,128)S(1)} %get-tuple-element.18), channel_id=1, source_target_pairs={{0,1},{1,0},{2,3},{3,2},{4,5},{5,4},{6,7},{7,6},{8,9},{9,8},{10,11... | collective-permute-start | bytes 221192 | tf_op jit(solution)/shard_map/ppermute | solution.py:323

commit v2 on v1

v2 whole, which is shorter than its diff:
```python
import functools
import math

import jax
import jax.numpy as jnp
from jax import lax
from jax.experimental import pallas as pl
from jax.experimental.pallas import tpu as pltpu
from jax.sharding import PartitionSpec as P

NDIR = 36
TIME_STEP = 0.5
CHUNKS = 3
GROUPS = 8
F32 = jnp.float32
BF16 = jnp.bfloat16
VMEM = pl.BlockSpec(memory_space=pltpu.VMEM)
SMEM = pl.BlockSpec(memory_space=pltpu.SMEM)
HBM = pl.BlockSpec(memory_space=pltpu.HBM)
ANY = pl.BlockSpec(memory_space=pl.ANY)


def call(kernel, mib, **kw):
    return pl.pallas_call(
        kernel,
        compiler_params=pltpu.CompilerParams(vmem_limit_bytes=mib * 1024 * 1024), **kw,
    )


def in_hbm(x):
    return pltpu.with_memory_space_constraint(x, pltpu.HBM)


def chunk_sizes(bins):
    tiles = bins // 128
    cuts = [tiles * i // CHUNKS for i in range(CHUNKS + 1)]
    return [(b - a) * 128 for a, b in zip(cuts, cuts[1:]) if b > a]


def prepare_kernel(energy, *refs):
    *parts, held, sems = refs
    piece = 128
    copies = []
    for i in range(held.shape[0] // (2 * piece)):
        at = pl.ds(2 * i * piece, 2 * piece)
        copies.append(pltpu.make_async_copy(energy.at[at, :], held.at[at, :], sems.at[i]))
        copies[-1].start()
    i = 0
    for part in parts:
        for k in range(0, part.shape[1], piece):
            copies[i].wait()
            for row in range(2):
                part[row, k : k + piece, :] = held[pl.ds(2 * i * piece + row, piece, stride=2), :].astype(BF16)
            i += 1


def gather_points(parts, points, start=0):
    for part in parts:
        size = part.shape[1]
        for row in range(2):
            points[pl.ds(start, size), row * 128 : (row + 1) * 128] = part[row]
        start += size


def blocks(band, mine, other, bins):
    size = bins // GROUPS
    half = bins // 2
    for j in range(GROUPS):
        weights, start = (mine, band * half) if j < GROUPS // 2 else (other, (1 - band) * half)
        k = j % (GROUPS // 2) * size
        yield j, weights, slice(k, k + size), pl.multiple_of(start + k, 16)


def dots(weights, rows, points, first=0):
    part = slice(first, first + points.shape[0])
    return [jnp.dot(weights[i, rows, part], points[...], preferred_element_type=F32) for i in range(2)]


def start_rows(source, target, sems, size):
    copies = []
    for j, k in enumerate(range(0, source.shape[1], size)):
        rows = pl.ds(k, size)
        copies.append(pltpu.make_async_copy(source.at[:, rows, :], target.at[:, rows, :], sems.at[j]))
        copies[-1].start()
    return copies


def gained(grow, gate):
    return TIME_STEP * (grow * jax.nn.sigmoid(gate))


def row_cells(row):
    return slice(row * 128, (row + 1) * 128)


def fill_tables(speed, direction, row_tables, col_tables):
    angle = (direction[...].astype(F32) + 0.5) * (2.0 * math.pi / NDIR)
    row_c, col_c = speed[...] * jnp.sin(angle), speed[...] * jnp.cos(angle)
    row_k, col_k = [0.5 * jnp.abs(c) * (1.0 - jnp.abs(c)) for c in (row_c, col_c)]
    col_k = jnp.where(col_c >= 0.0, col_k, -col_k)
    for tables, i, value in ((row_tables, 0, row_c), (row_tables, 1, row_k), (col_tables, 0, col_c), (col_tables, 1, col_k)):
        turned = value.T
        for r in range(value.shape[0]):
            tables[i, r * 128 : (r + 1) * 128, :] = jnp.broadcast_to(turned[:, r : r + 1], (128, 128))


def own_kernel(band_ref, mine, other, energy, out, points, held, here, field, energy_sems, in_sems, out_sems):
    bins = points.shape[0]
    size = bins // GROUPS
    energy_copies = []
    for i in range(bins // 128):
        at = pl.ds(256 * i, 256)
        energy_copies.append(pltpu.make_async_copy(energy.at[at, :], held.at[at, :], energy_sems.at[i]))
        energy_copies[-1].start()
    copies = start_rows(mine, here, in_sems, size)
    for i, copy in enumerate(energy_copies):
        copy.wait()
        for row in range(2):
            cells = held[pl.ds(256 * i + row, 128, stride=2), :].astype(BF16)
            points[128 * i : 128 * i + 128, row_cells(row)] = cells
    outs = []
    for j, weights, rows, at in blocks(band_ref[0], here, other, bins):
        if j < len(copies):
            copies[j].wait()
        src = gained(*dots(weights, rows, points))
        at = pl.ds(at, size)
        for row in range(2):
            field[row, at, :] = held[pl.ds(2 * at.start + row, size, stride=2), :] + src[:, row_cells(row)]
        outs.append(pltpu.make_async_copy(field.at[:, at, :], out.at[:, at, :], out_sems.at[j]))
        outs[-1].start()
    for copy in outs:
        copy.wait()


def near_kernel(band_ref, mine, other, own, speed, direction, *refs):
    *parts, field, here, own_here, row_tables, col_tables, points, in_sems, own_sem = refs
    bins = points.shape[0]
    size = bins // GROUPS
    copies = start_rows(mine, here, in_sems, size)
    own_copy = pltpu.make_async_copy(own, own_here, own_sem)
    own_copy.start()
    gather_points(parts, points)
    fill_tables(speed, direction, row_tables, col_tables)
    for j, weights, rows, at in blocks(band_ref[0], here, other, bins):
        if j < len(copies):
            copies[j].wait()
        src = gained(*dots(weights, rows, points))
        at = pl.ds(at, size)
        for row in range(2):
            field[row, at, :] = points[at, row_cells(row)].astype(F32) + src[:, row_cells(row)]
    own_copy.wait()


def inside_points(wide_ref, last, parts, points, start=0):
    w = wide_ref[0]
    inside = (w != 0) & (w != last)

    @pl.when(inside)
    def _():
        gather_points(parts, points, start)

    @pl.when(jnp.logical_not(inside))
    def _():
        size = sum(part.shape[1] for part in parts)
        points[pl.ds(start, size), :] = jnp.zeros((size, points.shape[1]), points.dtype)


def partial_kernel(last, band_ref, wide_ref, mine, other, *refs):
    *parts, sums, points = refs
    bins = sums.shape[1]
    inside_points(wide_ref, last, parts, points)
    for _, weights, rows, at in blocks(band_ref[0], mine, other, bins):
        for i, value in enumerate(dots(weights, rows, points)):
            sums[i, pl.ds(at, value.shape[0]), :] = value


def limited(a, b):
    return jnp.minimum(jnp.maximum(a, jnp.minimum(b, 0.0)), jnp.maximum(b, 0.0))


def row_kernel(last, band_ref, wide_ref, mine, other, sums, tables, own, near, *refs):
    *parts, field, edge, points, far = refs
    bins = points.shape[0]
    first = bins - parts[-1].shape[1]
    size = bins // GROUPS
    odd = lax.rem(wide_ref[0], 2)
    to_right = band_ref[0] == 0
    inside_points(wide_ref, last, parts, points)
    late = points.at[first:, :]
    lane = lax.broadcasted_iota(jnp.int32, (8, 128), 1)
    near_lane = jnp.where(to_right, 0, 127)
    near_roll = jnp.where(to_right, 1, 127)
    next_roll = jnp.where(to_right, 34, 30)

    def sweep(j, weights, rows, start, behind, ahead):
        group = lax.rem(band_ref[0] * (GROUPS // 2) + j, GROUPS)
        marks = [lane == ((near_lane + 2 * group + 32 * n) & 127) for n in range(4)]
        rolls = [(roll + 2 * group + 64 * row) & 127 for row in range(2) for roll in (near_roll, next_roll)]
        at = pl.ds(start, size)
        grow, gate = dots(weights, rows, late, first)
        src = gained(sums[0, at, :] + grow, sums[1, at, :] + gate)
        for row in range(2):
            far[row, at, :] = points[at, row_cells(row)].astype(F32) + src[:, row_cells(row)]
        for i in range(0, size, 8):
            here = pl.ds(pl.multiple_of(start + i, 8), 8)
            c, k = tables[0, here, :], tables[1, here, :]
            forward = c >= 0.0
            a = jnp.abs(c)
            q0, q1 = own[0, here, :], own[1, here, :]
            m2 = jnp.where(forward, behind[0, here, :], ahead[1, here, :])
            m1 = jnp.where(forward, behind[1, here, :], ahead[0, here, :])
            c0 = jnp.where(forward, q0, q1)
            c1 = jnp.where(forward, q1, q0)
            p2 = jnp.where(forward, ahead[0, here, :], behind[1, here, :])
            da, db, dc, dd = m1 - m2, c0 - m1, c1 - c0, p2 - c1
            fa = a * m1 + k * limited(db, da)
            fb = a * c0 + k * limited(dc, db)
            fc = a * c1 + k * limited(dd, dc)
            n0 = c0 - (fb - fa)
            n1 = c1 - (fc - fb)
            o0 = jnp.where(forward, n0, n1)
            o1 = jnp.where(forward, n1, n0)
            field[0, here, :] = o0
            field[1, here, :] = o1
            folded = edge[i : i + 8, :] if j else jnp.zeros_like(o0)
            for mark, roll, value in zip(marks, rolls, (o0, o0, o1, o1)):
                folded = jnp.where(mark, pltpu.roll(value, roll, axis=1), folded)
            edge[i : i + 8, :] = folded

    def run(behind, ahead):
        for j, weights, rows, start in blocks(band_ref[0], mine, other, bins):
            sweep(j, weights, rows, start, behind, ahead)

    @pl.when(odd == 1)
    def _():
        run(near, far)

    @pl.when(odd == 0)
    def _():
        run(far, near)


def col_kernel(band_ref, wide_ref, tables, sea, field, beside, out, held, sems):
    lane = lax.broadcasted_iota(jnp.int32, (8, 128), 1)
    first, last = lane == 0, lane == 127
    outer = first | last
    sign = (1 - 2 * band_ref[0]).astype(F32)
    bins = tables.shape[1]
    size = bins // GROUPS
    place = 2 * wide_ref[0]
    mask = [jnp.broadcast_to(sea[pl.ds(place + row, 1), :].astype(F32), (8, 128)) for row in range(2)]

    def cells(i, group):
        at = group * size + i
        here = slice(at, at + 8)
        c, k = tables[0, here, :], tables[1, here, :]
        forward = c >= 0.0
        a = jnp.abs(c)
        folded = beside[i : i + 8, :]
        h1 = pltpu.roll(folded, -2 * group % 128, axis=1) if group else folded
        h2 = pltpu.roll(folded, (-32 - 2 * group) % 128, axis=1)
        q0, q1 = field[0, here, :], field[1, here, :]
        ends = jnp.where(outer, q0, pltpu.roll(q1, 64, axis=1))
        ge = a * h1 + (sign * k) * limited(h1 - ends, h2 - h1)
        ends_at = (first & forward) | (last & jnp.logical_not(forward))
        for row, q in ((0, q0), (1, q1)):
            h, e = (h1, ge) if row == 0 else (pltpu.roll(h1, 64, axis=1), pltpu.roll(ge, 64, axis=1))
            d = jnp.where(last, h, pltpu.roll(q, 127, axis=1)) - q
            dm = jnp.where(first, q - h, pltpu.roll(d, 1, axis=1))
            g = a * q + k * limited(d, dm)
            t = jnp.where(forward, pltpu.roll(g, 1, axis=1), pltpu.roll(g, 127, axis=1))
            t = jnp.where(ends_at, e, t)
            held[pl.ds(2 * at + row, 8, stride=2), :] = (q - (g - t)) * mask[row]

    copies = []
    for group in range(GROUPS):
        for i in range(0, size, 8):
            cells(i, group)
        rows = pl.ds(2 * group * size, 2 * size)
        copies.append(pltpu.make_async_copy(held.at[rows, :], out.at[rows, :], sems.at[group]))
        copies[-1].start()
    for copy in copies:
        copy.wait()


def ring(count):
    order = list(range(0, count, 2)) + list(range(count - 1, 0, -2))
    return list(zip(order, order[1:] + order[:1]))


def local(energy, source_weights, speed, direction, sea_mask):
    bins, rows, cols = energy.shape
    wide, bands = lax.axis_size("wide"), lax.axis_size("band")
    if rows != 2 or cols != 128 or wide % 2 or bands != 2 or bins % (16 * GROUPS):
        raise ValueError("block shape")
    w_at = lax.axis_index("wide").astype(jnp.int32).reshape(1)
    b_at = lax.axis_index("band").astype(jnp.int32).reshape(1)
    flat = energy.reshape(bins * rows, cols)
    sizes = chunk_sizes(bins)
    swap = [(i, i ^ 1) for i in range(wide)]
    beside = [(i, i ^ 1) for i in range(bands)]

    other = lax.ppermute(source_weights, "band", beside)
    parts = call(
        prepare_kernel, 8,
        out_shape=[jax.ShapeDtypeStruct((2, n, cols), BF16) for n in sizes],
        in_specs=[HBM], out_specs=[VMEM] * len(sizes),
        scratch_shapes=[pltpu.VMEM((2 * bins, cols), F32), pltpu.SemaphoreType.DMA((bins // 128,))],
    )(in_hbm(flat))
    swapped, relayed = [], []
    for part in parts:
        swapped.append(lax.ppermute(part, "wide", swap))
    for part in swapped:
        relayed.append(lax.ppermute(part, "wide", ring(wide)))

    full = jax.ShapeDtypeStruct((2, bins, cols), F32)
    sums = jax.ShapeDtypeStruct((2, bins, 2 * cols), F32)
    points = pltpu.VMEM((bins, 2 * cols), BF16)
    n = len(sizes)
    table = jax.ShapeDtypeStruct((2, bins, cols), F32)
    half = jax.ShapeDtypeStruct(source_weights.shape, BF16)
    here = pltpu.VMEM(source_weights.shape, BF16)
    in_sems = pltpu.SemaphoreType.DMA((GROUPS // 2,))
    mine = in_hbm(source_weights)
    own = call(
        own_kernel, 9, out_shape=pltpu.HBM(full.shape, F32), in_specs=[SMEM, HBM, VMEM, HBM], out_specs=HBM,
        scratch_shapes=[points, pltpu.VMEM((2 * bins, cols), F32), here, pltpu.VMEM((2, bins, cols), F32),
                        pltpu.SemaphoreType.DMA((bins // 128,)), in_sems, pltpu.SemaphoreType.DMA((GROUPS,))],
    )(b_at, mine, other, in_hbm(flat))
    near, mine, own, row_tables, col_tables = call(
        near_kernel, 8, out_shape=[full, half, full, table, table],
        in_specs=[SMEM, HBM, VMEM, HBM] + [VMEM] * (2 + n), out_specs=[VMEM] * 5,
        scratch_shapes=[points, in_sems, pltpu.SemaphoreType.DMA],
    )(b_at, mine, other, in_hbm(own), speed.reshape(-1, 128), direction.reshape(-1, 128), *swapped)
    early = call(
        functools.partial(partial_kernel, wide - 1), 8, out_shape=sums,
        in_specs=[SMEM, SMEM] + [VMEM] * (1 + n), out_specs=VMEM,
        scratch_shapes=[pltpu.VMEM((bins - sizes[-1], 2 * cols), BF16)],
    )(b_at, w_at, mine, other, *relayed[:-1])
    field, edge = call(
        functools.partial(row_kernel, wide - 1), 10,
        out_shape=[full, jax.ShapeDtypeStruct((bins // GROUPS, cols), F32)],
        in_specs=[SMEM, SMEM] + [VMEM] * (6 + n), out_specs=[VMEM, VMEM],
        scratch_shapes=[points, pltpu.VMEM((2, bins, cols), F32)],
    )(b_at, w_at, mine, other, early, row_tables, own, near, *relayed)
    edges = lax.ppermute(edge, "band", beside)
    out = call(
        col_kernel, 10, out_shape=jax.ShapeDtypeStruct((bins * rows, cols), F32),
        in_specs=[SMEM, SMEM] + [VMEM] * 4, out_specs=HBM,
        scratch_shapes=[pltpu.VMEM((bins * rows, cols), F32), pltpu.SemaphoreType.DMA((GROUPS,))],
    )(b_at, w_at, col_tables, sea_mask, field, edges)
    return out.reshape(bins, rows, cols)


def solution(mesh):
    return jax.shard_map(
        local,
        mesh=mesh,
        in_specs=(
            P(None, ("grid", "wide"), "band"),
            P(None, "band", None),
            P(),
            P(),
            P("grid", "band"),
        ),
        out_specs=P(None, ("grid", "wide"), "band"),
        check_vma=False,
    )
```

time: 41.8 us -> 73.2 us (1.75)
  the two profiles are of different devices: /device:TPU:0 before, /device:TPU:9 now
where the time goes in v2:
time: 73.2 us; the launch traced here: 71.9 us
  Pallas kernels  52.5 us (72%)
  waiting for transfers between devices  10.6 us (14%)
  starting transfers between devices  8.51 us (12%)
    pallas_call x1, Pallas kernels, local(): call(col_kernel, 10, out_shape=jax.ShapeDtypeStruct((bins * rows, cols),...  37.6 us
    ppermute x3, waiting for transfers between devices, local(): swapped.append(lax.ppermute(part, 'wide', swap))  9.71 us
    pallas_call x1, Pallas kernels, local(): call(own_kernel, 9, out_shape=pltpu.HBM(full.shape, F32), in_specs=[SMEM,...  5.08 us
    pallas_call x1, Pallas kernels, local(): call(near_kernel, 8, out_shape=[full, half, full, table, table], in_specs...  4.46 us
    ppermute x3, starting transfers between devices, local(): relayed.append(lax.ppermute(part, 'wide', ring(wide)))  3.89 us
    pallas_call x1, Pallas kernels, local(): call(functools.partial(row_kernel, wide - 1), 10, out_shape=[full, jax.Sh...  2.78 us
    ppermute x3, starting transfers between devices, local(): swapped.append(lax.ppermute(part, 'wide', swap))  2.74 us
  transfers between devices with their start and end apart: 8, of which 4 were waited for; matrix products, arithmetic and copies ran while one was open for 0% of the time, Pallas kernels for 17%

profile of v2, /device:TPU:9, one launch (start us, length us, event | category | flops | bytes accessed | tf_op | source)
XLA Modules:
  0.0 71.9 jit_solution(9512015993466725138)
XLA Ops:
  0.0 0.7 collective-permute-start
  0.7 1.4 %shard_map.56 = (bf16[2,384,128]{2,1,0:T(8,128)(2,1)S(1)}, bf16[2,384,128]{2,1,0:T(8,128)(2,1)S(1)}, bf16[2,384,128]{2,1,0:T(8,128)(2,1)S(1)}) custom-call(f32[2304,128]{1,0:T(8,128)} %bitcast.8), custom_call_target="tpu_custom_call" | custom-call | tf_op jit(solution)/shard_map/pallas_call | solution.py:304
  2.1 1.3 %collective-permute-start.1 = (bf16[2,384,128]{2,1,0:T(8,128)(2,1)S(1)}, bf16[2,384,128]{2,1,0:T(8,128)(2,1)S(1)}, u32[]{:S(2)}, u32[]{:S(2)}) collective-permute-start(bf16[2,384,128]{2,1,0:T(8,128)(2,1)S(1)} %get-tuple-element.15), channel_id=1, source_target_pairs={{0,2},{2,0},{4,6},{6,4},{8,10},{10,8},{12,14},{14,12},{1,3},{3,1},... | collective-permute-start | bytes 589832 | tf_op jit(solution)/shard_map/ppermute | solution.py:312
  3.4 0.3 collective-permute-start.2
  3.6 1.2 %collective-permute-start.3 = (bf16[2,384,128]{2,1,0:T(8,128)(2,1)S(1)}, bf16[2,384,128]{2,1,0:T(8,128)(2,1)}, u32[]{:S(2)}, u32[]{:S(2)}) collective-permute-start(bf16[2,384,128]{2,1,0:T(8,128)(2,1)S(1)} %get-tuple-element.17), channel_id=1, source_target_pairs={{0,2},{2,0},{4,6},{6,4},{8,10},{10,8},{12,14},{14,12},{1,3},{3,1},... | collective-permute-start | bytes 589832 | tf_op jit(solution)/shard_map/ppermute | solution.py:312
  4.8 3.8 %collective-permute-done.1.refs_0_ = bf16[2,384,128]{2,1,0:T(8,128)(2,1)S(1)} collective-permute-done((bf16[2,384,128]{2,1,0:T(8,128)(2,1)S(1)}, bf16[2,384,128]{2,1,0:T(8,128)(2,1)S(1)}, u32[]{:S(2)}, u32[]{:S(2)}) %collective-permute-start.1) | collective-permute-done | bytes 196640 | tf_op jit(solution)/shard_map/ppermute | solution.py:312
  8.6 1.3 %collective-permute-start.4 = (bf16[2,384,128]{2,1,0:T(8,128)(2,1)S(1)}, bf16[2,384,128]{2,1,0:T(8,128)(2,1)S(1)}, u32[]{:S(2)}, u32[]{:S(2)}) collective-permute-start(bf16[2,384,128]{2,1,0:T(8,128)(2,1)S(1)} %collective-permute-done.1.refs_0_), channel_id=1, source_target_pairs={{0,4},{4,8},{8,12},{12,14},{14,10},{10,6},{6,2},{2,0},{1,5},{5,9},... | collective-permute-start | bytes 589832 | tf_op jit(solution)/shard_map/ppermute | solution.py:314
  9.9 2.9 %collective-permute-done.2.refs_1_ = bf16[2,384,128]{2,1,0:T(8,128)(2,1)S(1)} collective-permute-done((bf16[2,384,128]{2,1,0:T(8,128)(2,1)S(1)}, bf16[2,384,128]{2,1,0:T(8,128)(2,1)S(1)}, u32[]{:S(2)}, u32[]{:S(2)}) %collective-permute-start.2) | collective-permute-done | bytes 196640 | tf_op jit(solution)/shard_map/ppermute | solution.py:312
  12.8 1.3 %collective-permute-start.5 = (bf16[2,384,128]{2,1,0:T(8,128)(2,1)S(1)}, bf16[2,384,128]{2,1,0:T(8,128)(2,1)S(1)}, u32[]{:S(2)}, u32[]{:S(2)}) collective-permute-start(bf16[2,384,128]{2,1,0:T(8,128)(2,1)S(1)} %collective-permute-done.2.refs_1_), channel_id=1, source_target_pairs={{0,4},{4,8},{8,12},{12,14},{14,10},{10,6},{6,2},{2,0},{1,5},{5,9},... | collective-permute-start | bytes 589832 | tf_op jit(solution)/shard_map/ppermute | solution.py:314
  14.1 3.0 %collective-permute-done.3.refs_2_ = bf16[2,384,128]{2,1,0:T(8,128)(2,1)} collective-permute-done((bf16[2,384,128]{2,1,0:T(8,128)(2,1)S(1)}, bf16[2,384,128]{2,1,0:T(8,128)(2,1)}, u32[]{:S(2)}, u32[]{:S(2)}) %collective-permute-start.3) | collective-permute-done | bytes 196640 | tf_op jit(solution)/shard_map/ppermute | solution.py:312
  17.1 1.3 %collective-permute-start.6 = (bf16[2,384,128]{2,1,0:T(8,128)(2,1)}, bf16[2,384,128]{2,1,0:T(8,128)(2,1)}, u32[]{:S(2)}, u32[]{:S(2)}) collective-permute-start(bf16[2,384,128]{2,1,0:T(8,128)(2,1)} %collective-permute-done.3.refs_2_), channel_id=1, source_target_pairs={{0,4},{4,8},{8,12},{12,14},{14,10},{10,6},{6,2},{2,0},{1,5},{5,9},... | collective-permute-start | bytes 589832 | tf_op jit(solution)/shard_map/ppermute | solution.py:314
  18.4 0.0 collective-permute-done.other
  18.4 5.1 %shard_map.55.own = f32[2,1152,128]{2,1,0:T(8,128)} custom-call(s32[1]{0:T(128)} %bitcast.band_ref, bf16[2,576,1152]{2,1,0:T(8,128)(2,1)} %mine.3, bf16[2,576,1152]{2,1,0:T(8,128)(2,1)S(1)} %collective-permute-done.other, f32[2304,128]{1,0:T(8,128)} %bitcast.9), custom_call_target="tpu_custom_call" | custom-call | tf_op jit(solution)/shard_map/pallas_call | solution.py:325
  23.5 0.0 copy-done
  23.6 4.5 %shard_map.57 = (f32[2,1152,128]{2,1,0:T(8,128)S(1)}, bf16[2,576,1152]{2,1,0:T(8,128)(2,1)S(1)}, f32[2,1152,128]{2,1,0:T(8,128)S(1)}, f32[2,1152,128]{2,1,0:T(8,128)S(1)}, f32[2,1152,128]{2,1,0:T(8,128)S(1)}) custom-call(s32[1]{0:T(128)} %bitcast.band_ref, bf16[2,576,1152]{2,1,0:T(8,128)(2,1)} %mine.3, bf16[2,576,1152]{2,1,0:T(8,128)(2,1)S(1)} %collective-permute-done.other, ...), custom_call_target="tpu_custom_call" | custom-call | tf_op jit(solution)/shard_map/pallas_call | solution.py:330
  28.0 0.0 collective-permute-done.4.refs_0_
  28.0 0.0 collective-permute-done.5.refs_1_
  28.0 1.2 %shard_map.58.sums = f32[2,1152,256]{2,1,0:T(8,128)S(1)} custom-call(s32[1]{0:T(128)} %bitcast.band_ref, s32[1]{0:T(128)} %bitcast.1.wide_ref, bf16[2,576,1152]{2,1,0:T(8,128)(2,1)S(1)} %get-tuple-element.19.mine, bf16[2,576,1152]{2,1,0:T(8,128)(2,1)S(1)} %collective-permute-done.other, bf16[2,384,128]{2,1,0:T(8,128)(2,1)S(1)} %collective-permute-done.4.refs_0_, ...), custom_call_target="tpu_custom_call" | custom-call | tf_op jit(solution)/shard_map/pallas_call | solution.py:335
  29.2 0.0 collective-permute-done.6.refs_2_
  29.2 0.0 copy-start.2
  29.2 2.8 %shard_map.59 = (f32[2,1152,128]{2,1,0:T(8,128)S(1)}, f32[144,128]{1,0:T(8,128)S(1)}) custom-call(s32[1]{0:T(128)} %bitcast.band_ref, s32[1]{0:T(128)} %bitcast.1.wide_ref, bf16[2,576,1152]{2,1,0:T(8,128)(2,1)S(1)} %get-tuple-element.19.mine, bf16[2,576,1152]{2,1,0:T(8,128)(2,1)S(1)} %collective-permute-done.other, f32[2,1152,256]{2,1,0:T(8,128)S(1)} %shard_map.58.sums, ...), custom_call_target="tpu_custom_call" | custom-call | tf_op jit(solution)/shard_map/pallas_call | solution.py:340
  32.0 1.2 %collective-permute-start.7 = (f32[144,128]{1,0:T(8,128)S(1)}, f32[144,128]{1,0:T(8,128)S(1)}, u32[]{:S(2)}, u32[]{:S(2)}) collective-permute-start(f32[144,128]{1,0:T(8,128)S(1)} %get-tuple-element.24), channel_id=1, source_target_pairs={{0,1},{1,0},{2,3},{3,2},{4,5},{5,4},{6,7},{7,6},{8,9},{9,8},{10,11... | collective-permute-start | bytes 221192 | tf_op jit(solution)/shard_map/ppermute | solution.py:346
  33.2 0.9 %collective-permute-done.7.beside = f32[144,128]{1,0:T(8,128)S(1)} collective-permute-done((f32[144,128]{1,0:T(8,128)S(1)}, f32[144,128]{1,0:T(8,128)S(1)}, u32[]{:S(2)}, u32[]{:S(2)}) %collective-permute-start.7) | collective-permute-done | bytes 73760 | tf_op jit(solution)/shard_map/ppermute | solution.py:346
  34.1 37.6 %shard_map.60 = f32[2304,128]{1,0:T(8,128)} custom-call(s32[1]{0:T(128)} %bitcast.band_ref, s32[1]{0:T(128)} %bitcast.1.wide_ref, f32[2,1152,128]{2,1,0:T(8,128)S(1)} %get-tuple-element.18.tables, s32[16,128]{1,0:T(8,128)S(1)} %copy-done.2, f32[2,1152,128]{2,1,0:T(8,128)S(1)} %get-tuple-element.23.field, f32[144,128]{1,0:T(8,128)S(1)} %collective-permute-done.7.beside), custom_call_target="tpu_custom_call" | custom-call | tf_op jit(solution)/shard_map/pallas_call | solution.py:347
  (4 shorter events, 0.0 us)
Async XLA Ops:
  0.0 18.4 %collective-permute-start = (bf16[2,576,1152]{2,1,0:T(8,128)(2,1)}, bf16[2,576,1152]{2,1,0:T(8,128)(2,1)S(1)}, u32[]{:S(2)}, u32[]{:S(2)}) collective-permute-start(bf16[2,576,1152]{2,1,0:T(8,128)(2,1)} %mine.3), channel_id=1, source_target_pairs={{0,1},{1,0},{2,3},{3,2},{4,5},{5,4},{6,7},{7,6},{8,9},{9,8},{10,11... | collective-permute-start | bytes 7962632 | tf_op jit(solution)/shard_map/ppermute | solution.py:303
  2.1 6.5 %collective-permute-start.1 = (bf16[2,384,128]{2,1,0:T(8,128)(2,1)S(1)}, bf16[2,384,128]{2,1,0:T(8,128)(2,1)S(1)}, u32[]{:S(2)}, u32[]{:S(2)}) collective-permute-start(bf16[2,384,128]{2,1,0:T(8,128)(2,1)S(1)} %get-tuple-element.15), channel_id=1, source_target_pairs={{0,2},{2,0},{4,6},{6,4},{8,10},{10,8},{12,14},{14,12},{1,3},{3,1},... | collective-permute-start | bytes 589832 | tf_op jit(solution)/shard_map/ppermute | solution.py:312
  3.4 9.5 %collective-permute-start.2 = (bf16[2,384,128]{2,1,0:T(8,128)(2,1)S(1)}, bf16[2,384,128]{2,1,0:T(8,128)(2,1)S(1)}, u32[]{:S(2)}, u32[]{:S(2)}) collective-permute-start(bf16[2,384,128]{2,1,0:T(8,128)(2,1)S(1)} %get-tuple-element.16), channel_id=1, source_target_pairs={{0,2},{2,0},{4,6},{6,4},{8,10},{10,8},{12,14},{14,12},{1,3},{3,1},... | collective-permute-start | bytes 589832 | tf_op jit(solution)/shard_map/ppermute | solution.py:312
  3.6 13.5 %collective-permute-start.3 = (bf16[2,384,128]{2,1,0:T(8,128)(2,1)S(1)}, bf16[2,384,128]{2,1,0:T(8,128)(2,1)}, u32[]{:S(2)}, u32[]{:S(2)}) collective-permute-start(bf16[2,384,128]{2,1,0:T(8,128)(2,1)S(1)} %get-tuple-element.17), channel_id=1, source_target_pairs={{0,2},{2,0},{4,6},{6,4},{8,10},{10,8},{12,14},{14,12},{1,3},{3,1},... | collective-permute-start | bytes 589832 | tf_op jit(solution)/shard_map/ppermute | solution.py:312
  8.6 19.4 %collective-permute-start.4 = (bf16[2,384,128]{2,1,0:T(8,128)(2,1)S(1)}, bf16[2,384,128]{2,1,0:T(8,128)(2,1)S(1)}, u32[]{:S(2)}, u32[]{:S(2)}) collective-permute-start(bf16[2,384,128]{2,1,0:T(8,128)(2,1)S(1)} %collective-permute-done.1.refs_0_), channel_id=1, source_target_pairs={{0,4},{4,8},{8,12},{12,14},{14,10},{10,6},{6,2},{2,0},{1,5},{5,9},... | collective-permute-start | bytes 589832 | tf_op jit(solution)/shard_map/ppermute | solution.py:314
  12.8 15.2 %collective-permute-start.5 = (bf16[2,384,128]{2,1,0:T(8,128)(2,1)S(1)}, bf16[2,384,128]{2,1,0:T(8,128)(2,1)S(1)}, u32[]{:S(2)}, u32[]{:S(2)}) collective-permute-start(bf16[2,384,128]{2,1,0:T(8,128)(2,1)S(1)} %collective-permute-done.2.refs_1_), channel_id=1, source_target_pairs={{0,4},{4,8},{8,12},{12,14},{14,10},{10,6},{6,2},{2,0},{1,5},{5,9},... | collective-permute-start | bytes 589832 | tf_op jit(solution)/shard_map/ppermute | solution.py:314
  17.1 12.1 %collective-permute-start.6 = (bf16[2,384,128]{2,1,0:T(8,128)(2,1)}, bf16[2,384,128]{2,1,0:T(8,128)(2,1)}, u32[]{:S(2)}, u32[]{:S(2)}) collective-permute-start(bf16[2,384,128]{2,1,0:T(8,128)(2,1)} %collective-permute-done.3.refs_2_), channel_id=1, source_target_pairs={{0,4},{4,8},{8,12},{12,14},{14,10},{10,6},{6,2},{2,0},{1,5},{5,9},... | collective-permute-start | bytes 589832 | tf_op jit(solution)/shard_map/ppermute | solution.py:314
  18.4 5.1 %copy-start = (f32[1152]{0:T(1024)S(1)}, f32[1152]{0:T(1024)}, u32[]{:S(2)}) copy-start(f32[1152]{0:T(1024)} %param.7) | copy-start | bytes 13828
  18.4 5.1 %copy-start.1 = (s32[1152]{0:T(1024)S(1)}, s32[1152]{0:T(1024)}, u32[]{:S(2)}) copy-start(s32[1152]{0:T(1024)} %param.8) | copy-start | bytes 13828
  29.2 4.9 %copy-start.2 = (s32[16,128]{1,0:T(8,128)S(1)}, s32[16,128]{1,0:T(8,128)}, u32[]{:S(2)}) copy-start(s32[16,128]{1,0:T(8,128)} %sea.1) | copy-start | bytes 24580
  32.0 2.1 %collective-permute-start.7 = (f32[144,128]{1,0:T(8,128)S(1)}, f32[144,128]{1,0:T(8,128)S(1)}, u32[]{:S(2)}, u32[]{:S(2)}) collective-permute-start(f32[144,128]{1,0:T(8,128)S(1)} %get-tuple-element.24), channel_id=1, source_target_pairs={{0,1},{1,0},{2,3},{3,2},{4,5},{5,4},{6,7},{7,6},{8,9},{9,8},{10,11... | collective-permute-start | bytes 221192 | tf_op jit(solution)/shard_map/ppermute | solution.py:346

commit v3 on v2

v3 whole, which is shorter than its diff:
```python
import functools
import math

import jax
import jax.numpy as jnp
from jax import lax
from jax.experimental import pallas as pl
from jax.experimental.pallas import tpu as pltpu
from jax.sharding import PartitionSpec as P

NDIR = 36
TIME_STEP = 0.5
CHUNKS = 2
GROUPS = 8
STEP = 16
F32 = jnp.float32
BF16 = jnp.bfloat16
VMEM = pl.BlockSpec(memory_space=pltpu.VMEM)
SMEM = pl.BlockSpec(memory_space=pltpu.SMEM)
HBM = pl.BlockSpec(memory_space=pltpu.HBM)
ANY = pl.BlockSpec(memory_space=pl.ANY)


def call(kernel, mib, **kw):
    return pl.pallas_call(
        kernel,
        compiler_params=pltpu.CompilerParams(vmem_limit_bytes=mib * 1024 * 1024), **kw,
    )


def in_hbm(x):
    return pltpu.with_memory_space_constraint(x, pltpu.HBM)


def chunk_sizes(bins):
    tiles = bins // 128
    cuts = [-(-tiles * i // CHUNKS) for i in range(CHUNKS + 1)]
    return [(b - a) * 128 for a, b in zip(cuts, cuts[1:]) if b > a]


def prepare_kernel(start, energy, *refs):
    *parts, held, sems = refs
    piece = 128
    copies = []
    for i in range(held.shape[0] // (2 * piece)):
        from_at, to_at = pl.ds(2 * (start + i * piece), 2 * piece), pl.ds(2 * i * piece, 2 * piece)
        copies.append(pltpu.make_async_copy(energy.at[from_at, :], held.at[to_at, :], sems.at[i]))
        copies[-1].start()
    i = 0
    for part in parts:
        for k in range(0, part.shape[1], piece):
            copies[i].wait()
            for row in range(2):
                part[row, k : k + piece, :] = held[pl.ds(2 * i * piece + row, piece, stride=2), :].astype(BF16)
            i += 1


def points_copies(parts, points, sems):
    copies, start = [], 0
    for part in parts:
        size = part.shape[1]
        for row in range(2):
            target = points.at[pl.ds(start, size), row * 128 : (row + 1) * 128]
            copies.append(pltpu.make_async_copy(part.at[row], target, sems.at[len(copies)]))
        start += size
    return copies


def gather_points(parts, points, start=0):
    for part in parts:
        size = part.shape[1]
        for row in range(2):
            points[pl.ds(start, size), row * 128 : (row + 1) * 128] = part[row]
        start += size


def blocks(band, mine, other, bins):
    size = bins // GROUPS
    half = bins // 2
    for j in range(GROUPS):
        weights, start = (other, (1 - band) * half) if j < GROUPS // 2 else (mine, band * half)
        k = j % (GROUPS // 2) * size
        yield j, weights, slice(k, k + size), pl.multiple_of(start + k, 16)


def dots(weights, rows, points, first=0):
    part = slice(first, first + points.shape[0])
    return [jnp.dot(weights[i, rows, part], points[...], preferred_element_type=F32) for i in range(2)]


def start_rows(source, target, sems, size):
    copies = []
    for j, k in enumerate(range(0, source.shape[1], size)):
        rows = pl.ds(k, size)
        copies.append(pltpu.make_async_copy(source.at[:, rows, :], target.at[:, rows, :], sems.at[j]))
        copies[-1].start()
    return copies


def gained(grow, gate):
    return TIME_STEP * (grow * jax.nn.sigmoid(gate))


def row_cells(row):
    return slice(row * 128, (row + 1) * 128)


def table_kernel(speed, direction, row_out, col_out, row_table, col_table, sems):
    angle = (direction[...].astype(F32) + 0.5) * (2.0 * math.pi / NDIR)
    copies = []
    for n, (out, table, c) in enumerate((
        (row_out, row_table, speed[...] * jnp.sin(angle)), (col_out, col_table, speed[...] * jnp.cos(angle)),
    )):
        turned = c.T
        for r in range(c.shape[0]):
            table[r * 128 : (r + 1) * 128, :] = jnp.broadcast_to(turned[:, r : r + 1], (128, 128))
        copies.append(pltpu.make_async_copy(table, out, sems.at[n]))
        copies[-1].start()
    for copy in copies:
        copy.wait()


def own_kernel(band_ref, mine, other, energy, *refs):
    *parts, out, points, held, here, field, part_sems, in_sems, out_sems, energy_sem = refs
    bins = points.shape[0]
    size = bins // GROUPS
    given = points_copies(parts, points, part_sems)
    for copy in given:
        copy.start()
    energy_copy = pltpu.make_async_copy(energy, held, energy_sem)
    copies = start_rows(mine, here, in_sems, size)
    energy_copy.start()
    for copy in given:
        copy.wait()
    outs = []

    def finish(start):
        at = pl.ds(start, size)
        for row in range(2):
            field[row, at, :] = field[row, at, :] + held[pl.ds(2 * start + row, size, stride=2), :]
        outs.append(pltpu.make_async_copy(field.at[:, at, :], out.at[:, at, :], out_sems.at[len(outs)]))
        outs[-1].start()

    waiting = []
    for j, weights, rows, start in blocks(band_ref[0], here, other, bins):
        if j >= GROUPS - len(copies):
            copies[j - GROUPS + len(copies)].wait()
        src = gained(*dots(weights, rows, points))
        for row in range(2):
            field[row, pl.ds(start, size), :] = src[:, row_cells(row)]
        waiting.append(start)
        if j == GROUPS // 2:
            energy_copy.wait()
        if j >= GROUPS // 2:
            for item in waiting:
                finish(item)
            waiting = []
    for copy in outs:
        copy.wait()


def near_kernel(band_ref, mine, other, own, *refs):
    *parts, late, field, here, own_here, points, late_here, in_sems, own_sem, late_sem = refs
    bins = points.shape[0]
    size = bins // GROUPS
    split = bins - late.shape[1]
    late_copy = pltpu.make_async_copy(late, late_here, late_sem)
    late_copy.start()
    copies = start_rows(mine, here, in_sems, size)
    own_copy = pltpu.make_async_copy(own, own_here, own_sem)
    own_copy.start()
    gather_points(parts, points)
    early = []
    for j, weights, rows, start in blocks(band_ref[0], here, other, bins):
        if j < 2:
            early.append(dots(weights, rows, points.at[:split, :]))
    late_copy.wait()
    gather_points([late_here], points, split)
    for j, weights, rows, start in blocks(band_ref[0], here, other, bins):
        if j >= GROUPS - len(copies):
            copies[j - GROUPS + len(copies)].wait()
        if j < len(early):
            src = gained(*[x + y for x, y in zip(early[j], dots(weights, rows, points.at[split:, :], split))])
        else:
            src = gained(*dots(weights, rows, points))
        at = pl.ds(start, size)
        for row in range(2):
            field[row, at, :] = points[at, row_cells(row)].astype(F32) + src[:, row_cells(row)]
    own_copy.wait()


def inside_points(wide_ref, last, parts, points, start=0):
    w = wide_ref[0]
    inside = (w != 0) & (w != last)

    @pl.when(inside)
    def _():
        gather_points(parts, points, start)

    @pl.when(jnp.logical_not(inside))
    def _():
        size = sum(part.shape[1] for part in parts)
        points[pl.ds(start, size), :] = jnp.zeros((size, points.shape[1]), points.dtype)


def partial_kernel(last, band_ref, wide_ref, mine, other, *refs):
    *parts, sums, points = refs
    bins = sums.shape[1]
    inside_points(wide_ref, last, parts, points)
    for _, weights, rows, at in blocks(band_ref[0], mine, other, bins):
        for i, value in enumerate(dots(weights, rows, points)):
            sums[i, pl.ds(at, value.shape[0]), :] = value


def limited(a, b):
    return jnp.minimum(jnp.maximum(a, jnp.minimum(b, 0.0)), jnp.maximum(b, 0.0))


def row_kernel(last, band_ref, wide_ref, mine, other, sums, courants, own, near, *refs):
    *parts, field, edge, points, far = refs
    bins = points.shape[0]
    first = bins - parts[-1].shape[1]
    size = bins // GROUPS
    odd = lax.rem(wide_ref[0], 2)
    to_right = band_ref[0] == 0
    inside_points(wide_ref, last, parts, points)
    late = points.at[first:, :]
    lane = lax.broadcasted_iota(jnp.int32, (8, 128), 1)
    edge_lane = jnp.where(to_right, 126, 0)

    def sweep(j, weights, rows, start, behind, ahead):
        group = lax.rem((1 - band_ref[0]) * (GROUPS // 2) + j, GROUPS)
        turns = [4 * (group + GROUPS * row) for row in range(2)]
        marks = [((lane - edge_lane - turn) & 127) < 2 for turn in turns]
        at = pl.ds(start, size)
        grow, gate = dots(weights, rows, late, first)
        src = gained(sums[0, at, :] + grow, sums[1, at, :] + gate)
        for row in range(2):
            far[row, at, :] = points[at, row_cells(row)].astype(F32) + src[:, row_cells(row)]
        for i in range(0, size, 8):
            here = pl.ds(pl.multiple_of(start + i, 8), 8)
            c = courants[here, :]
            forward = c >= 0.0
            a = jnp.abs(c)
            k = 0.5 * a * (1.0 - a)
            q0, q1 = own[0, here, :], own[1, here, :]
            m2 = jnp.where(forward, behind[0, here, :], ahead[1, here, :])
            m1 = jnp.where(forward, behind[1, here, :], ahead[0, here, :])
            c0 = jnp.where(forward, q0, q1)
            c1 = jnp.where(forward, q1, q0)
            p2 = jnp.where(forward, ahead[0, here, :], behind[1, here, :])
            da, db, dc, dd = m1 - m2, c0 - m1, c1 - c0, p2 - c1
            fa = a * m1 + k * limited(db, da)
            fb = a * c0 + k * limited(dc, db)
            fc = a * c1 + k * limited(dd, dc)
            n0 = c0 - (fb - fa)
            n1 = c1 - (fc - fb)
            o0 = jnp.where(forward, n0, n1)
            o1 = jnp.where(forward, n1, n0)
            field[0, here, :] = o0
            field[1, here, :] = o1
            folded = edge[i : i + 8, :] if j else jnp.zeros_like(o0)
            for mark, turn, value in zip(marks, turns, (o0, o1)):
                folded = jnp.where(mark, pltpu.roll(value, turn, axis=1), folded)
            edge[i : i + 8, :] = folded

    def run(behind, ahead):
        for j, weights, rows, start in blocks(band_ref[0], mine, other, bins):
            sweep(j, weights, rows, start, behind, ahead)

    @pl.when(odd == 1)
    def _():
        run(near, far)

    @pl.when(odd == 0)
    def _():
        run(far, near)


def col_kernel(wide_ref, courants, sea, field, beside, out, held, sems):
    size = beside.shape[0]
    place = 2 * wide_ref[0]
    lane = lax.broadcasted_iota(jnp.int32, (GROUPS, STEP, 128), 2)
    low, high, first, last = lane < 2, lane >= 126, lane == 0, lane == 127
    mask = [jnp.broadcast_to(sea[pl.ds(place + row, 1), :].astype(F32), (STEP, 128)) for row in range(2)]

    def roll(x, by):
        return pltpu.roll(x, by % 128, axis=2)

    def body(i, carry):
        i = pl.multiple_of(i * STEP, STEP)
        here = pl.ds(i, STEP)
        folded = beside[here, :]
        c = courants[:, here, :]
        forward = c >= 0.0
        a = jnp.abs(c)
        k = 0.5 * a * (1.0 - a)
        halos = [jnp.stack([pltpu.roll(folded, -4 * (group + GROUPS * row) % 128, axis=1)
                            if group + row else folded for group in range(GROUPS)]) for row in range(2)]
        cells = [field[row, :, here, :] for row in range(2)]
        shifted = [(roll(jnp.where(last, halo, q), 1), roll(jnp.where(high, halo, q), 2),
                    roll(jnp.where(first, halo, q), -1), roll(jnp.where(low, halo, q), -2))
                   for halo, q in zip(halos, cells)]
        for row, (q, (l1, l2, r1, r2)) in enumerate(zip(cells, shifted)):
            m2 = jnp.where(forward, l2, r2)
            m1 = jnp.where(forward, l1, r1)
            p1 = jnp.where(forward, r1, l1)
            da, db, dc = m1 - m2, q - m1, p1 - q
            fa = a * m1 + k * limited(db, da)
            fb = a * q + k * limited(dc, db)
            new = (q - (fb - fa)) * mask[row]
            for group in range(GROUPS):
                held[pl.ds(2 * (group * size + i) + row, STEP, stride=2), :] = new[group]
        return carry

    copies = []
    step = size // 3
    for part in range(3):
        lax.fori_loop(part * step // STEP, (part + 1) * step // STEP, body, 0)
        for group in range(GROUPS):
            rows = pl.ds(2 * (group * size + part * step), 2 * step)
            copies.append(pltpu.make_async_copy(held.at[rows, :], out.at[rows, :], sems.at[len(copies)]))
            copies[-1].start()
    for copy in copies:
        copy.wait()


def relay_pairs(count, apart):
    up, down = list(range(0, count, 2)), list(range(count - 1, 0, -2))
    rings = [up, down] if apart else [up + down]
    return [pair for order in rings for pair in zip(order, order[1:] + order[:1])]


def local(energy, source_weights, speed, direction, sea_mask):
    bins, rows, cols = energy.shape
    wide, bands = lax.axis_size("wide"), lax.axis_size("band")
    if rows != 2 or cols != 128 or wide % 2 or bands != 2 or bins % (48 * GROUPS):
        raise ValueError("block shape")
    w_at = lax.axis_index("wide").astype(jnp.int32).reshape(1)
    b_at = lax.axis_index("band").astype(jnp.int32).reshape(1)
    flat = energy.reshape(bins * rows, cols)
    sizes = chunk_sizes(bins)
    swap = [(i, i ^ 1) for i in range(wide)]
    beside = [(i, i ^ 1) for i in range(bands)]

    other = lax.ppermute(source_weights, "band", beside)

    def prepare(start, these):
        total = sum(these)
        return call(
            functools.partial(prepare_kernel, start), 8,
            out_shape=[jax.ShapeDtypeStruct((2, n, cols), BF16) for n in these],
            in_specs=[HBM], out_specs=[VMEM] * len(these),
            scratch_shapes=[pltpu.VMEM((2 * total, cols), F32), pltpu.SemaphoreType.DMA((total // 128,))],
        )(in_hbm(flat))

    parts = prepare(0, sizes[:1]) + prepare(sizes[0], sizes[1:])
    swapped, relayed = [], []
    for part in parts:
        swapped.append(lax.ppermute(part, "wide", swap))
    for i, part in enumerate(swapped):
        relayed.append(lax.ppermute(part, "wide", relay_pairs(wide, i < len(sizes) - 1)))

    full = jax.ShapeDtypeStruct((2, bins, cols), F32)
    sums = jax.ShapeDtypeStruct((2, bins, 2 * cols), F32)
    points = pltpu.VMEM((bins, 2 * cols), BF16)
    n = len(sizes)
    table = jax.ShapeDtypeStruct((bins, cols), F32)
    half = jax.ShapeDtypeStruct(source_weights.shape, BF16)
    here = pltpu.VMEM(source_weights.shape, BF16)
    in_sems = pltpu.SemaphoreType.DMA((GROUPS // 2,))
    mine = in_hbm(source_weights)
    own = in_hbm(call(
        own_kernel, 9, out_shape=pltpu.HBM(full.shape, F32), in_specs=[SMEM, HBM, VMEM, HBM] + [ANY] * n,
        out_specs=HBM,
        scratch_shapes=[points, pltpu.VMEM((2 * bins, cols), F32), here, pltpu.VMEM(full.shape, F32),
                        pltpu.SemaphoreType.DMA((2 * n,)), in_sems, pltpu.SemaphoreType.DMA((GROUPS,)),
                        pltpu.SemaphoreType.DMA],
    )(b_at, mine, other, in_hbm(flat), *parts))
    row_courants, col_courants = call(
        table_kernel, 4, out_shape=[pltpu.HBM(table.shape, F32)] * 2,
        in_specs=[VMEM] * 2, out_specs=[HBM] * 2,
        scratch_shapes=[pltpu.VMEM(table.shape, F32)] * 2 + [pltpu.SemaphoreType.DMA((2,))],
    )(speed.reshape(-1, 128), direction.reshape(-1, 128))
    near, mine, own = call(
        near_kernel, 8, out_shape=[full, half, full],
        in_specs=[SMEM, HBM, VMEM, HBM] + [VMEM] * (n - 1) + [HBM], out_specs=[VMEM] * 3,
        scratch_shapes=[points, pltpu.VMEM((2, sizes[-1], cols), BF16), in_sems,
                        pltpu.SemaphoreType.DMA, pltpu.SemaphoreType.DMA],
    )(b_at, mine, other, own, *swapped[:-1], in_hbm(swapped[-1]))
    early = call(
        functools.partial(partial_kernel, wide - 1), 8, out_shape=sums,
        in_specs=[SMEM, SMEM] + [VMEM] * (1 + n), out_specs=VMEM,
        scratch_shapes=[pltpu.VMEM((bins - sizes[-1], 2 * cols), BF16)],
    )(b_at, w_at, mine, other, *relayed[:-1])
    field, edge = call(
        functools.partial(row_kernel, wide - 1), 10,
        out_shape=[full, jax.ShapeDtypeStruct((bins // GROUPS, cols), F32)],
        in_specs=[SMEM, SMEM] + [VMEM] * (6 + n), out_specs=[VMEM, VMEM],
        scratch_shapes=[points, pltpu.VMEM((2, bins, cols), F32)],
    )(b_at, w_at, mine, other, early, row_courants, own, near, *relayed)
    edges = lax.ppermute(edge, "band", beside)
    out = call(
        col_kernel, 10, out_shape=jax.ShapeDtypeStruct((bins * rows, cols), F32),
        in_specs=[SMEM] + [VMEM] * 4, out_specs=HBM,
        scratch_shapes=[pltpu.VMEM((bins * rows, cols), F32), pltpu.SemaphoreType.DMA((3 * GROUPS,))],
    )(w_at, col_courants.reshape(GROUPS, -1, cols), sea_mask, field.reshape(2, GROUPS, -1, cols), edges)
    return out.reshape(bins, rows, cols)


def solution(mesh):
    return jax.shard_map(
        local,
        mesh=mesh,
        in_specs=(
            P(None, ("grid", "wide"), "band"),
            P(None, "band", None),
            P(),
            P(),
            P("grid", "band"),
        ),
        out_specs=P(None, ("grid", "wide"), "band"),
        check_vma=False,
    )
```

time: 73.2 us -> 41 us (0.56)
  the two profiles are of different devices: /device:TPU:9 before, /device:TPU:0 now
where the time goes in v3:
time: 41 us; the launch traced here: 40.8 us
  Pallas kernels  20.5 us (50%)
  waiting for transfers between devices  11.3 us (28%)
  starting transfers between devices  7.11 us (17%)
  local copies, waits for them, and re-layouts  1.66 us (4%)
    ppermute x2, waiting for transfers between devices, local(): swapped.append(lax.ppermute(part, 'wide', swap))  10.1 us
    pallas_call x1, Pallas kernels, local(): call(near_kernel, 8, out_shape=[full, half, full], in_specs=[SMEM, HBM, V...  5.07 us
    pallas_call x1, Pallas kernels, local(): call(own_kernel, 9, out_shape=pltpu.HBM(full.shape, F32), in_specs=[SMEM,...  4.21 us
    ppermute x2, starting transfers between devices, local(): lax.ppermute(part, 'wide', relay_pairs(wide, i < len(sizes) - 1))  3.93 us
    pallas_call x1, Pallas kernels, local(): call(col_kernel, 10, out_shape=jax.ShapeDtypeStruct((bins * rows, cols),...  3.65 us
    pallas_call x1, Pallas kernels, local(): call(functools.partial(row_kernel, wide - 1), 10, out_shape=[full, jax.Sh...  2.63 us
    ppermute x2, starting transfers between devices, local(): swapped.append(lax.ppermute(part, 'wide', swap))  2.63 us
    pallas_call x2, Pallas kernels, prepare(): call(functools.partial(prepare_kernel, start), 8, out_shape=[jax.ShapeDty...  2.37 us
  transfers between devices with their start and end apart: 6, of which 3 were waited for; matrix products, arithmetic and copies ran while one was open for 0% of the time, Pallas kernels for 35%

profile of v3, /device:TPU:0, one launch (start us, length us, event | category | flops | bytes accessed | tf_op | source)
XLA Modules:
  0.0 40.8 jit_solution(17692154068589620208)
XLA Ops:
  0.0 0.5 %collective-permute-start = (bf16[2,576,1152]{2,1,0:T(8,128)(2,1)}, bf16[2,576,1152]{2,1,0:T(8,128)(2,1)S(1)}, u32[]{:S(2)}, u32[]{:S(2)}) collective-permute-start(bf16[2,576,1152]{2,1,0:T(8,128)(2,1)} %mine.3), channel_id=1, source_target_pairs={{0,1},{1,0},{2,3},{3,2},{4,5},{5,4},{6,7},{7,6},{8,9},{9,8},{10,11... | collective-permute-start | bytes 7962632 | tf_op jit(solution)/shard_map/ppermute | solution.py:346
  0.5 1.2 %shard_map.56.refs_0_ = bf16[2,640,128]{2,1,0:T(8,128)(2,1)S(1)} custom-call(f32[2304,128]{1,0:T(8,128)} %bitcast.12), custom_call_target="tpu_custom_call" | custom-call | tf_op jit(solution)/shard_map/pallas_call | solution.py:350
  1.7 2.5 %collective-permute-start.1 = (bf16[2,640,128]{2,1,0:T(8,128)(2,1)S(1)}, bf16[2,640,128]{2,1,0:T(8,128)(2,1)}, u32[]{:S(2)}, u32[]{:S(2)}) collective-permute-start(bf16[2,640,128]{2,1,0:T(8,128)(2,1)S(1)} %shard_map.56.refs_0_), channel_id=1, source_target_pairs={{0,2},{2,0},{4,6},{6,4},{8,10},{10,8},{12,14},{14,12},{1,3},{3,1},... | collective-permute-start | bytes 983048 | tf_op jit(solution)/shard_map/ppermute | solution.py:360
  4.3 1.1 %shard_map.57.refs_1_ = bf16[2,512,128]{2,1,0:T(8,128)(2,1)S(1)} custom-call(f32[2304,128]{1,0:T(8,128)} %bitcast.13), custom_call_target="tpu_custom_call" | custom-call | tf_op jit(solution)/shard_map/pallas_call | solution.py:350
  5.4 0.1 collective-permute-start.2
  5.5 0.7 %copy-done = bf16[2,512,128]{2,1,0:T(8,128)(2,1)} copy-done((bf16[2,512,128]{2,1,0:T(8,128)(2,1)}, bf16[2,512,128]{2,1,0:T(8,128)(2,1)S(1)}, u32[]{:S(2)}) %copy-start) | copy-done | bytes 262168
  6.2 6.7 %collective-permute-done.1.refs_0_ = bf16[2,640,128]{2,1,0:T(8,128)(2,1)} collective-permute-done((bf16[2,640,128]{2,1,0:T(8,128)(2,1)S(1)}, bf16[2,640,128]{2,1,0:T(8,128)(2,1)}, u32[]{:S(2)}, u32[]{:S(2)}) %collective-permute-start.1) | collective-permute-done | bytes 327712 | tf_op jit(solution)/shard_map/ppermute | solution.py:360
  13.0 2.1 %collective-permute-start.3 = (bf16[2,640,128]{2,1,0:T(8,128)(2,1)}, bf16[2,640,128]{2,1,0:T(8,128)(2,1)S(1)}, u32[]{:S(2)}, u32[]{:S(2)}) collective-permute-start(bf16[2,640,128]{2,1,0:T(8,128)(2,1)} %collective-permute-done.1.refs_0_), channel_id=1, source_target_pairs={{0,4},{4,8},{8,12},{12,0},{14,10},{10,6},{6,2},{2,14},{1,5},{5,9},... | collective-permute-start | bytes 983048 | tf_op jit(solution)/shard_map/ppermute | solution.py:362
  15.1 3.3 %collective-permute-done.2.refs_1_ = bf16[2,512,128]{2,1,0:T(8,128)(2,1)} collective-permute-done((bf16[2,512,128]{2,1,0:T(8,128)(2,1)S(1)}, bf16[2,512,128]{2,1,0:T(8,128)(2,1)}, u32[]{:S(2)}, u32[]{:S(2)}) %collective-permute-start.2) | collective-permute-done | bytes 262176 | tf_op jit(solution)/shard_map/ppermute | solution.py:360
  18.4 1.8 %collective-permute-start.4 = (bf16[2,512,128]{2,1,0:T(8,128)(2,1)}, bf16[2,512,128]{2,1,0:T(8,128)(2,1)}, u32[]{:S(2)}, u32[]{:S(2)}) collective-permute-start(bf16[2,512,128]{2,1,0:T(8,128)(2,1)} %collective-permute-done.2.refs_1_), channel_id=1, source_target_pairs={{0,4},{4,8},{8,12},{12,14},{14,10},{10,6},{6,2},{2,0},{1,5},{5,9},... | collective-permute-start | bytes 786440 | tf_op jit(solution)/shard_map/ppermute | solution.py:362
  20.2 1.5 %shard_map.55 = (f32[1152,128]{1,0:T(8,128)}, f32[1152,128]{1,0:T(8,128)}) custom-call(f32[9,128]{1,0:T(8,128)S(1)} %bitcast.10, s32[9,128]{1,0:T(8,128)S(1)} %bitcast.11), custom_call_target="tpu_custom_call" | custom-call | tf_op jit(solution)/shard_map/pallas_call | solution.py:380
  21.7 0.0 collective-permute-done.other
  21.7 0.0 copy-start.1
  21.7 0.9 %copy-done.1 = bf16[2,512,128]{2,1,0:T(8,128)(2,1)S(1)} copy-done((bf16[2,512,128]{2,1,0:T(8,128)(2,1)S(1)}, bf16[2,512,128]{2,1,0:T(8,128)(2,1)}, u32[]{:S(2)}) %copy-start.1) | copy-done | bytes 262168
  22.7 4.2 %shard_map.58.own = f32[2,1152,128]{2,1,0:T(8,128)} custom-call(s32[1]{0:T(128)} %bitcast.4.band_ref, bf16[2,576,1152]{2,1,0:T(8,128)(2,1)} %mine.3, bf16[2,576,1152]{2,1,0:T(8,128)(2,1)S(1)} %collective-permute-done.other, f32[2304,128]{1,0:T(8,128)} %bitcast.14, bf16[2,640,128]{2,1,0:T(8,128)(2,1)S(1)} %shard_map.56.refs_0_, bf16[2,512,128]{2,1,0:T(8,128)(2,1)S(1)} %copy-done.1), custom_call_target="tpu_custom_call" | custom-call | tf_op jit(solution)/shard_map/pallas_call | solution.py:373
  26.9 5.1 %shard_map.59 = (f32[2,1152,128]{2,1,0:T(8,128)S(1)}, bf16[2,576,1152]{2,1,0:T(8,128)(2,1)S(1)}, f32[2,1152,128]{2,1,0:T(8,128)S(1)}) custom-call(s32[1]{0:T(128)} %bitcast.4.band_ref, bf16[2,576,1152]{2,1,0:T(8,128)(2,1)} %mine.3, bf16[2,576,1152]{2,1,0:T(8,128)(2,1)S(1)} %collective-permute-done.other, f32[2,1152,128]{2,1,0:T(8,128)} %shard_map.58.own, ...), custom_call_target="tpu_custom_call" | custom-call | tf_op jit(solution)/shard_map/pallas_call | solution.py:385
  32.0 0.0 collective-permute-done.3.refs_0_
  32.0 1.1 %shard_map.60.sums = f32[2,1152,256]{2,1,0:T(8,128)S(1)} custom-call(s32[1]{0:T(128)} %bitcast.4.band_ref, s32[1]{0:T(128)} %bitcast.wide_ref, bf16[2,576,1152]{2,1,0:T(8,128)(2,1)S(1)} %get-tuple-element.13.mine, bf16[2,576,1152]{2,1,0:T(8,128)(2,1)S(1)} %collective-permute-done.other, bf16[2,640,128]{2,1,0:T(8,128)(2,1)S(1)} %collective-permute-done.3.refs_0_), custom_call_target="tpu_custom_call" | custom-call | tf_op jit(solution)/shard_map/pallas_call | solution.py:391
  33.1 0.0 collective-permute-done.4.refs_1_
  33.1 0.0 copy-start.4
  33.2 2.6 %shard_map.61 = (f32[2,1152,128]{2,1,0:T(8,128)S(1)}, f32[144,128]{1,0:T(8,128)S(1)}) custom-call(s32[1]{0:T(128)} %bitcast.4.band_ref, s32[1]{0:T(128)} %bitcast.wide_ref, bf16[2,576,1152]{2,1,0:T(8,128)(2,1)S(1)} %get-tuple-element.13.mine, bf16[2,576,1152]{2,1,0:T(8,128)(2,1)S(1)} %collective-permute-done.other, f32[2,1152,256]{2,1,0:T(8,128)S(1)} %shard_map.60.sums, ...), custom_call_target="tpu_custom_call" | custom-call | tf_op jit(solution)/shard_map/pallas_call | solution.py:396
  35.8 0.1 collective-permute-start.5
  35.9 1.3 %collective-permute-done.5.beside = f32[144,128]{1,0:T(8,128)S(1)} collective-permute-done((f32[144,128]{1,0:T(8,128)S(1)}, f32[144,128]{1,0:T(8,128)S(1)}, u32[]{:S(2)}, u32[]{:S(2)}) %collective-permute-start.5) | collective-permute-done | bytes 73760 | tf_op jit(solution)/shard_map/ppermute | solution.py:402
  37.1 3.6 %shard_map.62 = f32[2304,128]{1,0:T(8,128)} custom-call(s32[1]{0:T(128)} %bitcast.wide_ref, f32[8,144,128]{2,1,0:T(8,128)S(1)} %bitcast.9, s32[16,128]{1,0:T(8,128)S(1)} %copy-done.4, f32[2,8,144,128]{3,2,1,0:T(8,128)S(1)} %bitcast.8, f32[144,128]{1,0:T(8,128)S(1)} %collective-permute-done.5.beside), custom_call_target="tpu_custom_call" | custom-call | tf_op jit(solution)/shard_map/pallas_call | solution.py:403
  (10 shorter events, 0.0 us)
Async XLA Ops:
  0.0 21.7 %collective-permute-start = (bf16[2,576,1152]{2,1,0:T(8,128)(2,1)}, bf16[2,576,1152]{2,1,0:T(8,128)(2,1)S(1)}, u32[]{:S(2)}, u32[]{:S(2)}) collective-permute-start(bf16[2,576,1152]{2,1,0:T(8,128)(2,1)} %mine.3), channel_id=1, source_target_pairs={{0,1},{1,0},{2,3},{3,2},{4,5},{5,4},{6,7},{7,6},{8,9},{9,8},{10,11... | collective-permute-start | bytes 7962632 | tf_op jit(solution)/shard_map/ppermute | solution.py:346
  0.5 19.7 %copy-start.5 = (f32[1152]{0:T(1024)S(1)}, f32[1152]{0:T(1024)}, u32[]{:S(2)}) copy-start(f32[1152]{0:T(1024)} %param.7) | copy-start | bytes 13828
  0.5 19.7 %copy-start.6 = (s32[1152]{0:T(1024)S(1)}, s32[1152]{0:T(1024)}, u32[]{:S(2)}) copy-start(s32[1152]{0:T(1024)} %param.8) | copy-start | bytes 13828
  1.7 11.2 %collective-permute-start.1 = (bf16[2,640,128]{2,1,0:T(8,128)(2,1)S(1)}, bf16[2,640,128]{2,1,0:T(8,128)(2,1)}, u32[]{:S(2)}, u32[]{:S(2)}) collective-permute-start(bf16[2,640,128]{2,1,0:T(8,128)(2,1)S(1)} %shard_map.56.refs_0_), channel_id=1, source_target_pairs={{0,2},{2,0},{4,6},{6,4},{8,10},{10,8},{12,14},{14,12},{1,3},{3,1},... | collective-permute-start | bytes 983048 | tf_op jit(solution)/shard_map/ppermute | solution.py:360
  5.4 13.0 %collective-permute-start.2 = (bf16[2,512,128]{2,1,0:T(8,128)(2,1)S(1)}, bf16[2,512,128]{2,1,0:T(8,128)(2,1)}, u32[]{:S(2)}, u32[]{:S(2)}) collective-permute-start(bf16[2,512,128]{2,1,0:T(8,128)(2,1)S(1)} %shard_map.57.refs_1_), channel_id=1, source_target_pairs={{0,2},{2,0},{4,6},{6,4},{8,10},{10,8},{12,14},{14,12},{1,3},{3,1},... | collective-permute-start | bytes 786440 | tf_op jit(solution)/shard_map/ppermute | solution.py:360
  5.5 0.7 %copy-start = (bf16[2,512,128]{2,1,0:T(8,128)(2,1)}, bf16[2,512,128]{2,1,0:T(8,128)(2,1)S(1)}, u32[]{:S(2)}) copy-start(bf16[2,512,128]{2,1,0:T(8,128)(2,1)S(1)} %shard_map.57.refs_1_) | copy-start | bytes 786436
  13.0 19.0 %collective-permute-start.3 = (bf16[2,640,128]{2,1,0:T(8,128)(2,1)}, bf16[2,640,128]{2,1,0:T(8,128)(2,1)S(1)}, u32[]{:S(2)}, u32[]{:S(2)}) collective-permute-start(bf16[2,640,128]{2,1,0:T(8,128)(2,1)} %collective-permute-done.1.refs_0_), channel_id=1, source_target_pairs={{0,4},{4,8},{8,12},{12,0},{14,10},{10,6},{6,2},{2,14},{1,5},{5,9},... | collective-permute-start | bytes 983048 | tf_op jit(solution)/shard_map/ppermute | solution.py:362
  18.4 14.7 %collective-permute-start.4 = (bf16[2,512,128]{2,1,0:T(8,128)(2,1)}, bf16[2,512,128]{2,1,0:T(8,128)(2,1)}, u32[]{:S(2)}, u32[]{:S(2)}) collective-permute-start(bf16[2,512,128]{2,1,0:T(8,128)(2,1)} %collective-permute-done.2.refs_1_), channel_id=1, source_target_pairs={{0,4},{4,8},{8,12},{12,14},{14,10},{10,6},{6,2},{2,0},{1,5},{5,9},... | collective-permute-start | bytes 786440 | tf_op jit(solution)/shard_map/ppermute | solution.py:362
  21.7 1.0 %copy-start.1 = (bf16[2,512,128]{2,1,0:T(8,128)(2,1)S(1)}, bf16[2,512,128]{2,1,0:T(8,128)(2,1)}, u32[]{:S(2)}) copy-start(bf16[2,512,128]{2,1,0:T(8,128)(2,1)} %copy-done) | copy-start | bytes 786436
  32.0 1.1 %copy-start.2 = (f32[1152,128]{1,0:T(8,128)S(1)}, f32[1152,128]{1,0:T(8,128)}, u32[]{:S(2)}) copy-start(f32[1152,128]{1,0:T(8,128)} %get-tuple-element.14.courants) | copy-start | bytes 1769476
  33.1 4.0 %copy-start.3 = (f32[1152,128]{1,0:T(8,128)S(1)}, f32[1152,128]{1,0:T(8,128)}, u32[]{:S(2)}) copy-start(f32[1152,128]{1,0:T(8,128)} %get-tuple-element.12) | copy-start | bytes 1769476
  33.1 4.0 %copy-start.4 = (s32[16,128]{1,0:T(8,128)S(1)}, s32[16,128]{1,0:T(8,128)}, u32[]{:S(2)}) copy-start(s32[16,128]{1,0:T(8,128)} %sea.1) | copy-start | bytes 24580
  35.8 1.3 %collective-permute-start.5 = (f32[144,128]{1,0:T(8,128)S(1)}, f32[144,128]{1,0:T(8,128)S(1)}, u32[]{:S(2)}, u32[]{:S(2)}) collective-permute-start(f32[144,128]{1,0:T(8,128)S(1)} %get-tuple-element.18), channel_id=1, source_target_pairs={{0,1},{1,0},{2,3},{3,2},{4,5},{5,4},{6,7},{7,6},{8,9},{9,8},{10,11... | collective-permute-start | bytes 221192 | tf_op jit(solution)/shard_map/ppermute | solution.py:402

commit v4 on v3

--- a/solution.py
+++ b/solution.py
@@ -11,6 +11,7 @@
 NDIR = 36
 TIME_STEP = 0.5
 CHUNKS = 2
+PIECE = 64
 GROUPS = 8
 STEP = 16
 F32 = jnp.float32
@@ -33,14 +34,14 @@
 
 
 def chunk_sizes(bins):
-    tiles = bins // 128
-    cuts = [-(-tiles * i // CHUNKS) for i in range(CHUNKS + 1)]
-    return [(b - a) * 128 for a, b in zip(cuts, cuts[1:]) if b > a]
+    tiles = bins // 64
+    cuts = [tiles * i // CHUNKS for i in range(CHUNKS + 1)]
+    return [(b - a) * 64 for a, b in zip(cuts, cuts[1:])]
 
 
 def prepare_kernel(start, energy, *refs):
     *parts, held, sems = refs
-    piece = 128
+    piece = PIECE
     copies = []
     for i in range(held.shape[0] // (2 * piece)):
         from_at, to_at = pl.ds(2 * (start + i * piece), 2 * piece), pl.ds(2 * i * piece, 2 * piece)
@@ -351,7 +352,7 @@
             functools.partial(prepare_kernel, start), 8,
             out_shape=[jax.ShapeDtypeStruct((2, n, cols), BF16) for n in these],
             in_specs=[HBM], out_specs=[VMEM] * len(these),
-            scratch_shapes=[pltpu.VMEM((2 * total, cols), F32), pltpu.SemaphoreType.DMA((total // 128,))],
+            scratch_shapes=[pltpu.VMEM((2 * total, cols), F32), pltpu.SemaphoreType.DMA((total // PIECE,))],
         )(in_hbm(flat))
 
     parts = prepare(0, sizes[:1]) + prepare(sizes[0], sizes[1:])
@@ -393,6 +394,7 @@
         in_specs=[SMEM, SMEM] + [VMEM] * (1 + n), out_specs=VMEM,
         scratch_shapes=[pltpu.VMEM((bins - sizes[-1], 2 * cols), BF16)],
     )(b_at, w_at, mine, other, *relayed[:-1])
+    relayed[-1] = pltpu.with_memory_space_constraint(relayed[-1], pltpu.VMEM)
     field, edge = call(
         functools.partial(row_kernel, wide - 1), 10,
         out_shape=[full, jax.ShapeDtypeStruct((bins // GROUPS, cols), F32)],

time: 41 us -> 40.5 us (0.988)
  local copies, waits for them, and re-layouts: 1.66 us -> 0.02 us
  waiting for transfers between devices: 11.3 us -> 12 us
    unnamed x14 -> x10, local copies, waits for them, and re-layouts: 1.66 us -> 0.02 us
    ppermute x2, waiting for transfers between devices: 10.1 us -> 10.7 us  [local(): swapped.append(lax.ppermute(part, 'wide', swap))]
  transfers between devices with their start and end apart: 6 -> 6, of which waited for: 3 -> 3; matrix products, arithmetic and copies ran while one was open for 0% -> 0% of each run, Pallas kernels for 35% -> 36%
where the time goes in v4:
time: 40.5 us; the launch traced here: 40.2 us
  Pallas kernels  20.9 us (52%)
  waiting for transfers between devices  12 us (30%)
  starting transfers between devices  7.12 us (18%)
    ppermute x2, waiting for transfers between devices, local(): swapped.append(lax.ppermute(part, 'wide', swap))  10.7 us
    pallas_call x1, Pallas kernels, local(): call(near_kernel, 8, out_shape=[full, half, full], in_specs=[SMEM, HBM, V...  5.17 us
    pallas_call x1, Pallas kernels, local(): call(own_kernel, 9, out_shape=pltpu.HBM(full.shape, F32), in_specs=[SMEM,...  4.21 us
    ppermute x2, starting transfers between devices, local(): lax.ppermute(part, 'wide', relay_pairs(wide, i < len(sizes) - 1))  3.93 us
    pallas_call x1, Pallas kernels, local(): call(col_kernel, 10, out_shape=jax.ShapeDtypeStruct((bins * rows, cols),...  3.65 us
    pallas_call x1, Pallas kernels, local(): call(functools.partial(row_kernel, wide - 1), 10, out_shape=[full, jax.Sh...  2.92 us
    ppermute x2, starting transfers between devices, local(): swapped.append(lax.ppermute(part, 'wide', swap))  2.63 us
    pallas_call x2, Pallas kernels, prepare(): call(functools.partial(prepare_kernel, start), 8, out_shape=[jax.ShapeDty...  2.37 us
  transfers between devices with their start and end apart: 6, of which 3 were waited for; matrix products, arithmetic and copies ran while one was open for 0% of the time, Pallas kernels for 36%

profile of v4, /device:TPU:0, one launch (start us, length us, event | category | flops | bytes accessed | tf_op | source)
XLA Modules:
  0.0 40.2 jit_solution(9307570120083071137)
XLA Ops:
  0.0 0.5 %collective-permute-start = (bf16[2,576,1152]{2,1,0:T(8,128)(2,1)}, bf16[2,576,1152]{2,1,0:T(8,128)(2,1)S(1)}, u32[]{:S(2)}, u32[]{:S(2)}) collective-permute-start(bf16[2,576,1152]{2,1,0:T(8,128)(2,1)} %mine.3), channel_id=1, source_target_pairs={{0,1},{1,0},{2,3},{3,2},{4,5},{5,4},{6,7},{7,6},{8,9},{9,8},{10,11... | collective-permute-start | bytes 7962632 | tf_op jit(solution)/shard_map/ppermute | solution.py:347
  0.5 1.2 %shard_map.56.refs_0_ = bf16[2,576,128]{2,1,0:T(8,128)(2,1)S(1)} custom-call(f32[2304,128]{1,0:T(8,128)} %bitcast.12), custom_call_target="tpu_custom_call" | custom-call | tf_op jit(solution)/shard_map/pallas_call | solution.py:351
  1.7 2.5 %collective-permute-start.1 = (bf16[2,576,128]{2,1,0:T(8,128)(2,1)S(1)}, bf16[2,576,128]{2,1,0:T(8,128)(2,1)}, u32[]{:S(2)}, u32[]{:S(2)}) collective-permute-start(bf16[2,576,128]{2,1,0:T(8,128)(2,1)S(1)} %shard_map.56.refs_0_), channel_id=1, source_target_pairs={{0,2},{2,0},{4,6},{6,4},{8,10},{10,8},{12,14},{14,12},{1,3},{3,1},... | collective-permute-start | bytes 884744 | tf_op jit(solution)/shard_map/ppermute | solution.py:361
  4.2 1.2 %shard_map.57.refs_1_ = bf16[2,576,128]{2,1,0:T(8,128)(2,1)S(1)} custom-call(f32[2304,128]{1,0:T(8,128)} %bitcast.13), custom_call_target="tpu_custom_call" | custom-call | tf_op jit(solution)/shard_map/pallas_call | solution.py:351
  5.4 0.1 collective-permute-start.2
  5.5 6.7 %collective-permute-done.1.refs_0_ = bf16[2,576,128]{2,1,0:T(8,128)(2,1)} collective-permute-done((bf16[2,576,128]{2,1,0:T(8,128)(2,1)S(1)}, bf16[2,576,128]{2,1,0:T(8,128)(2,1)}, u32[]{:S(2)}, u32[]{:S(2)}) %collective-permute-start.1) | collective-permute-done | bytes 294944 | tf_op jit(solution)/shard_map/ppermute | solution.py:361
  12.2 2.1 %collective-permute-start.3 = (bf16[2,576,128]{2,1,0:T(8,128)(2,1)}, bf16[2,576,128]{2,1,0:T(8,128)(2,1)S(1)}, u32[]{:S(2)}, u32[]{:S(2)}) collective-permute-start(bf16[2,576,128]{2,1,0:T(8,128)(2,1)} %collective-permute-done.1.refs_0_), channel_id=1, source_target_pairs={{0,4},{4,8},{8,12},{12,0},{14,10},{10,6},{6,2},{2,14},{1,5},{5,9},... | collective-permute-start | bytes 884744 | tf_op jit(solution)/shard_map/ppermute | solution.py:363
  14.3 4.0 %collective-permute-done.2.refs_1_ = bf16[2,576,128]{2,1,0:T(8,128)(2,1)} collective-permute-done((bf16[2,576,128]{2,1,0:T(8,128)(2,1)S(1)}, bf16[2,576,128]{2,1,0:T(8,128)(2,1)}, u32[]{:S(2)}, u32[]{:S(2)}) %collective-permute-start.2) | collective-permute-done | bytes 294944 | tf_op jit(solution)/shard_map/ppermute | solution.py:361
  18.4 1.8 %collective-permute-start.4 = (bf16[2,576,128]{2,1,0:T(8,128)(2,1)}, bf16[2,576,128]{2,1,0:T(8,128)(2,1)}, u32[]{:S(2)}, u32[]{:S(2)}) collective-permute-start(bf16[2,576,128]{2,1,0:T(8,128)(2,1)} %collective-permute-done.2.refs_1_), channel_id=1, source_target_pairs={{0,4},{4,8},{8,12},{12,14},{14,10},{10,6},{6,2},{2,0},{1,5},{5,9},... | collective-permute-start | bytes 884744 | tf_op jit(solution)/shard_map/ppermute | solution.py:363
  20.2 0.0 copy-done.3
  20.2 0.0 copy-done.4
  20.2 1.5 %shard_map.55 = (f32[1152,128]{1,0:T(8,128)}, f32[1152,128]{1,0:T(8,128)}) custom-call(f32[9,128]{1,0:T(8,128)S(1)} %bitcast.10, s32[9,128]{1,0:T(8,128)S(1)} %bitcast.11), custom_call_target="tpu_custom_call" | custom-call | tf_op jit(solution)/shard_map/pallas_call | solution.py:381
  21.7 0.0 collective-permute-done.other
  21.7 4.2 %shard_map.58.own = f32[2,1152,128]{2,1,0:T(8,128)} custom-call(s32[1]{0:T(128)} %bitcast.4.band_ref, bf16[2,576,1152]{2,1,0:T(8,128)(2,1)} %mine.3, bf16[2,576,1152]{2,1,0:T(8,128)(2,1)S(1)} %collective-permute-done.other, f32[2304,128]{1,0:T(8,128)} %bitcast.14, bf16[2,576,128]{2,1,0:T(8,128)(2,1)S(1)} %shard_map.56.refs_0_, ...), custom_call_target="tpu_custom_call" | custom-call | tf_op jit(solution)/shard_map/pallas_call | solution.py:374
  25.9 5.2 %shard_map.59 = (f32[2,1152,128]{2,1,0:T(8,128)S(1)}, bf16[2,576,1152]{2,1,0:T(8,128)(2,1)S(1)}, f32[2,1152,128]{2,1,0:T(8,128)S(1)}) custom-call(s32[1]{0:T(128)} %bitcast.4.band_ref, bf16[2,576,1152]{2,1,0:T(8,128)(2,1)} %mine.3, bf16[2,576,1152]{2,1,0:T(8,128)(2,1)S(1)} %collective-permute-done.other, f32[2,1152,128]{2,1,0:T(8,128)} %shard_map.58.own, ...), custom_call_target="tpu_custom_call" | custom-call | tf_op jit(solution)/shard_map/pallas_call | solution.py:386
  31.1 0.0 collective-permute-done.3.refs_0_
  31.1 0.0 copy-start
  31.1 1.1 %shard_map.60.sums = f32[2,1152,256]{2,1,0:T(8,128)S(1)} custom-call(s32[1]{0:T(128)} %bitcast.4.band_ref, s32[1]{0:T(128)} %bitcast.wide_ref, bf16[2,576,1152]{2,1,0:T(8,128)(2,1)S(1)} %get-tuple-element.13.mine, bf16[2,576,1152]{2,1,0:T(8,128)(2,1)S(1)} %collective-permute-done.other, bf16[2,576,128]{2,1,0:T(8,128)(2,1)S(1)} %collective-permute-done.3.refs_0_), custom_call_target="tpu_custom_call" | custom-call | tf_op jit(solution)/shard_map/pallas_call | solution.py:392
  32.2 0.0 collective-permute-done.4.refs_1_
  32.3 0.0 copy-start.2
  32.3 2.9 %shard_map.61 = (f32[2,1152,128]{2,1,0:T(8,128)S(1)}, f32[144,128]{1,0:T(8,128)S(1)}) custom-call(s32[1]{0:T(128)} %bitcast.4.band_ref, s32[1]{0:T(128)} %bitcast.wide_ref, bf16[2,576,1152]{2,1,0:T(8,128)(2,1)S(1)} %get-tuple-element.13.mine, bf16[2,576,1152]{2,1,0:T(8,128)(2,1)S(1)} %collective-permute-done.other, f32[2,1152,256]{2,1,0:T(8,128)S(1)} %shard_map.60.sums, ...), custom_call_target="tpu_custom_call" | custom-call | tf_op jit(solution)/shard_map/pallas_call | solution.py:398
  35.2 0.1 collective-permute-start.5
  35.3 1.3 %collective-permute-done.5.beside = f32[144,128]{1,0:T(8,128)S(1)} collective-permute-done((f32[144,128]{1,0:T(8,128)S(1)}, f32[144,128]{1,0:T(8,128)S(1)}, u32[]{:S(2)}, u32[]{:S(2)}) %collective-permute-start.5) | collective-permute-done | bytes 73760 | tf_op jit(solution)/shard_map/ppermute | solution.py:404
  36.5 3.6 %shard_map.62 = f32[2304,128]{1,0:T(8,128)} custom-call(s32[1]{0:T(128)} %bitcast.wide_ref, f32[8,144,128]{2,1,0:T(8,128)S(1)} %bitcast.9, s32[16,128]{1,0:T(8,128)S(1)} %copy-done.2, f32[2,8,144,128]{3,2,1,0:T(8,128)S(1)} %bitcast.8, f32[144,128]{1,0:T(8,128)S(1)} %collective-permute-done.5.beside), custom_call_target="tpu_custom_call" | custom-call | tf_op jit(solution)/shard_map/pallas_call | solution.py:405
  (6 shorter events, 0.0 us)
Async XLA Ops:
  0.0 21.7 %collective-permute-start = (bf16[2,576,1152]{2,1,0:T(8,128)(2,1)}, bf16[2,576,1152]{2,1,0:T(8,128)(2,1)S(1)}, u32[]{:S(2)}, u32[]{:S(2)}) collective-permute-start(bf16[2,576,1152]{2,1,0:T(8,128)(2,1)} %mine.3), channel_id=1, source_target_pairs={{0,1},{1,0},{2,3},{3,2},{4,5},{5,4},{6,7},{7,6},{8,9},{9,8},{10,11... | collective-permute-start | bytes 7962632 | tf_op jit(solution)/shard_map/ppermute | solution.py:347
  0.5 19.7 %copy-start.3 = (f32[1152]{0:T(1024)S(1)}, f32[1152]{0:T(1024)}, u32[]{:S(2)}) copy-start(f32[1152]{0:T(1024)} %param.7) | copy-start | bytes 13828
  0.5 19.7 %copy-start.4 = (s32[1152]{0:T(1024)S(1)}, s32[1152]{0:T(1024)}, u32[]{:S(2)}) copy-start(s32[1152]{0:T(1024)} %param.8) | copy-start | bytes 13828
  1.7 10.5 %collective-permute-start.1 = (bf16[2,576,128]{2,1,0:T(8,128)(2,1)S(1)}, bf16[2,576,128]{2,1,0:T(8,128)(2,1)}, u32[]{:S(2)}, u32[]{:S(2)}) collective-permute-start(bf16[2,576,128]{2,1,0:T(8,128)(2,1)S(1)} %shard_map.56.refs_0_), channel_id=1, source_target_pairs={{0,2},{2,0},{4,6},{6,4},{8,10},{10,8},{12,14},{14,12},{1,3},{3,1},... | collective-permute-start | bytes 884744 | tf_op jit(solution)/shard_map/ppermute | solution.py:361
  5.4 12.9 %collective-permute-start.2 = (bf16[2,576,128]{2,1,0:T(8,128)(2,1)S(1)}, bf16[2,576,128]{2,1,0:T(8,128)(2,1)}, u32[]{:S(2)}, u32[]{:S(2)}) collective-permute-start(bf16[2,576,128]{2,1,0:T(8,128)(2,1)S(1)} %shard_map.57.refs_1_), channel_id=1, source_target_pairs={{0,2},{2,0},{4,6},{6,4},{8,10},{10,8},{12,14},{14,12},{1,3},{3,1},... | collective-permute-start | bytes 884744 | tf_op jit(solution)/shard_map/ppermute | solution.py:361
  12.2 18.9 %collective-permute-start.3 = (bf16[2,576,128]{2,1,0:T(8,128)(2,1)}, bf16[2,576,128]{2,1,0:T(8,128)(2,1)S(1)}, u32[]{:S(2)}, u32[]{:S(2)}) collective-permute-start(bf16[2,576,128]{2,1,0:T(8,128)(2,1)} %collective-permute-done.1.refs_0_), channel_id=1, source_target_pairs={{0,4},{4,8},{8,12},{12,0},{14,10},{10,6},{6,2},{2,14},{1,5},{5,9},... | collective-permute-start | bytes 884744 | tf_op jit(solution)/shard_map/ppermute | solution.py:363
  18.4 13.9 %collective-permute-start.4 = (bf16[2,576,128]{2,1,0:T(8,128)(2,1)}, bf16[2,576,128]{2,1,0:T(8,128)(2,1)}, u32[]{:S(2)}, u32[]{:S(2)}) collective-permute-start(bf16[2,576,128]{2,1,0:T(8,128)(2,1)} %collective-permute-done.2.refs_1_), channel_id=1, source_target_pairs={{0,4},{4,8},{8,12},{12,14},{14,10},{10,6},{6,2},{2,0},{1,5},{5,9},... | collective-permute-start | bytes 884744 | tf_op jit(solution)/shard_map/ppermute | solution.py:363
  31.1 1.1 %copy-start = (f32[1152,128]{1,0:T(8,128)S(1)}, f32[1152,128]{1,0:T(8,128)}, u32[]{:S(2)}) copy-start(f32[1152,128]{1,0:T(8,128)} %get-tuple-element.14.courants) | copy-start | bytes 1769476
  32.3 4.3 %copy-start.1 = (f32[1152,128]{1,0:T(8,128)S(1)}, f32[1152,128]{1,0:T(8,128)}, u32[]{:S(2)}) copy-start(f32[1152,128]{1,0:T(8,128)} %get-tuple-element.12) | copy-start | bytes 1769476
  32.3 4.3 %copy-start.2 = (s32[16,128]{1,0:T(8,128)S(1)}, s32[16,128]{1,0:T(8,128)}, u32[]{:S(2)}) copy-start(s32[16,128]{1,0:T(8,128)} %sea.1) | copy-start | bytes 24580
  35.2 1.3 %collective-permute-start.5 = (f32[144,128]{1,0:T(8,128)S(1)}, f32[144,128]{1,0:T(8,128)S(1)}, u32[]{:S(2)}, u32[]{:S(2)}) collective-permute-start(f32[144,128]{1,0:T(8,128)S(1)} %get-tuple-element.18), channel_id=1, source_target_pairs={{0,1},{1,0},{2,3},{3,2},{4,5},{5,4},{6,7},{7,6},{8,9},{9,8},{10,11... | collective-permute-start | bytes 221192 | tf_op jit(solution)/shard_map/ppermute | solution.py:404

commit v5 on v4

--- a/solution.py
+++ b/solution.py
@@ -227,12 +227,13 @@
     inside_points(wide_ref, last, parts, points)
     late = points.at[first:, :]
     lane = lax.broadcasted_iota(jnp.int32, (8, 128), 1)
-    edge_lane = jnp.where(to_right, 126, 0)
+    edge_lane = jnp.where(to_right, 0, 4)
 
     def sweep(j, weights, rows, start, behind, ahead):
         group = lax.rem((1 - band_ref[0]) * (GROUPS // 2) + j, GROUPS)
-        turns = [4 * (group + GROUPS * row) for row in range(2)]
-        marks = [((lane - edge_lane - turn) & 127) < 2 for turn in turns]
+        slots = [8 * (group + GROUPS * row) for row in range(2)]
+        turns = [slot + 4 & 127 for slot in slots]
+        marks = [((lane - edge_lane - slot) & 127) < 4 for slot in slots]
         at = pl.ds(start, size)
         grow, gate = dots(weights, rows, late, first)
         src = gained(sums[0, at, :] + grow, sums[1, at, :] + gate)
@@ -278,50 +279,63 @@
         run(far, near)
 
 
-def col_kernel(wide_ref, courants, sea, field, beside, out, held, sems):
-    size = beside.shape[0]
+def sea_rows(wide_ref, sea, size):
     place = 2 * wide_ref[0]
+    return [jnp.broadcast_to(sea[pl.ds(place + row, 1), :].astype(F32), (size, 128)) for row in range(2)]
+
+
+def along_lanes(c, q, l1, l2, r1, r2):
+    forward = c >= 0.0
+    a = jnp.abs(c)
+    k = 0.5 * a * (1.0 - a)
+    m2 = jnp.where(forward, l2, r2)
+    m1 = jnp.where(forward, l1, r1)
+    p1 = jnp.where(forward, r1, l1)
+    da, db, dc = m1 - m2, q - m1, p1 - q
+    fa = a * m1 + k * limited(db, da)
+    fb = a * q + k * limited(dc, db)
+    return q - (fb - fa)
+
+
+def col_kernel(wide_ref, courants, sea, field, out):
     lane = lax.broadcasted_iota(jnp.int32, (GROUPS, STEP, 128), 2)
     low, high, first, last = lane < 2, lane >= 126, lane == 0, lane == 127
-    mask = [jnp.broadcast_to(sea[pl.ds(place + row, 1), :].astype(F32), (STEP, 128)) for row in range(2)]
-
-    def roll(x, by):
-        return pltpu.roll(x, by % 128, axis=2)
+    mask = sea_rows(wide_ref, sea, STEP)
+
+    def roll(ends, q, by):
+        return pltpu.roll(jnp.where(ends, 0.0, q), by % 128, axis=2)
 
     def body(i, carry):
-        i = pl.multiple_of(i * STEP, STEP)
-        here = pl.ds(i, STEP)
-        folded = beside[here, :]
+        here = pl.ds(pl.multiple_of(i * STEP, STEP), STEP)
         c = courants[:, here, :]
-        forward = c >= 0.0
-        a = jnp.abs(c)
-        k = 0.5 * a * (1.0 - a)
-        halos = [jnp.stack([pltpu.roll(folded, -4 * (group + GROUPS * row) % 128, axis=1)
-                            if group + row else folded for group in range(GROUPS)]) for row in range(2)]
         cells = [field[row, :, here, :] for row in range(2)]
-        shifted = [(roll(jnp.where(last, halo, q), 1), roll(jnp.where(high, halo, q), 2),
-                    roll(jnp.where(first, halo, q), -1), roll(jnp.where(low, halo, q), -2))
-                   for halo, q in zip(halos, cells)]
-        for row, (q, (l1, l2, r1, r2)) in enumerate(zip(cells, shifted)):
-            m2 = jnp.where(forward, l2, r2)
-            m1 = jnp.where(forward, l1, r1)
-            p1 = jnp.where(forward, r1, l1)
-            da, db, dc = m1 - m2, q - m1, p1 - q
-            fa = a * m1 + k * limited(db, da)
-            fb = a * q + k * limited(dc, db)
-            new = (q - (fb - fa)) * mask[row]
-            for group in range(GROUPS):
-                held[pl.ds(2 * (group * size + i) + row, STEP, stride=2), :] = new[group]
+        shifted = [(roll(last, q, 1), roll(high, q, 2), roll(first, q, -1), roll(low, q, -2)) for q in cells]
+        for row in range(2):
+            out[row, :, here, :] = along_lanes(c, cells[row], *shifted[row]) * mask[row]
         return carry
 
+    lax.fori_loop(0, field.shape[2] // STEP, body, 0)
+
+
+def border_kernel(band_ref, wide_ref, courants, sea, swept, edge, beside, out, held, sems):
+    size = edge.shape[0]
+    lane = lax.broadcasted_iota(jnp.int32, (size, 128), 1)
+    mask = sea_rows(wide_ref, sea, size)
+    cells = edge[...] + beside[...]
+    c = courants[0]
+    for group in range(1, GROUPS):
+        c = jnp.where((lane >> 3) % GROUPS == group, courants[group], c)
+    new = along_lanes(c, cells, *[pltpu.roll(cells, by % 128, axis=1) for by in (1, 2, -1, -2)])
+    border = ((lane + jnp.where(band_ref[0] == 0, 2, 0)) & 127) < 2
     copies = []
-    step = size // 3
-    for part in range(3):
-        lax.fori_loop(part * step // STEP, (part + 1) * step // STEP, body, 0)
-        for group in range(GROUPS):
-            rows = pl.ds(2 * (group * size + part * step), 2 * step)
-            copies.append(pltpu.make_async_copy(held.at[rows, :], out.at[rows, :], sems.at[len(copies)]))
-            copies[-1].start()
+    for group in range(GROUPS):
+        for row in range(2):
+            here = pltpu.roll(new, -(8 * (group + GROUPS * row) + 4) % 128, axis=1)
+            value = jnp.where(border, here * mask[row], swept[row, group])
+            held[pl.ds(2 * group * size + row, size, stride=2), :] = value
+        rows = pl.ds(2 * group * size, 2 * size)
+        copies.append(pltpu.make_async_copy(held.at[rows, :], out.at[rows, :], sems.at[group]))
+        copies[-1].start()
     for copy in copies:
         copy.wait()
 
@@ -402,11 +416,17 @@
         scratch_shapes=[points, pltpu.VMEM((2, bins, cols), F32)],
     )(b_at, w_at, mine, other, early, row_courants, own, near, *relayed)
     edges = lax.ppermute(edge, "band", beside)
+    grouped = (2, GROUPS, bins // GROUPS, cols)
+    col_courants = col_courants.reshape(grouped[1:])
+    swept = call(
+        col_kernel, 6, out_shape=jax.ShapeDtypeStruct(grouped, F32),
+        in_specs=[SMEM] + [VMEM] * 3, out_specs=VMEM,
+    )(w_at, col_courants, sea_mask, field.reshape(grouped))
     out = call(
-        col_kernel, 10, out_shape=jax.ShapeDtypeStruct((bins * rows, cols), F32),
-        in_specs=[SMEM] + [VMEM] * 4, out_specs=HBM,
-        scratch_shapes=[pltpu.VMEM((bins * rows, cols), F32), pltpu.SemaphoreType.DMA((3 * GROUPS,))],
-    )(w_at, col_courants.reshape(GROUPS, -1, cols), sea_mask, field.reshape(2, GROUPS, -1, cols), edges)
+        border_kernel, 6, out_shape=jax.ShapeDtypeStruct((bins * rows, cols), F32),
+        in_specs=[SMEM, SMEM] + [VMEM] * 5, out_specs=HBM,
+        scratch_shapes=[pltpu.VMEM((bins * rows, cols), F32), pltpu.SemaphoreType.DMA((GROUPS,))],
+    )(b_at, w_at, col_courants, sea_mask, swept, edge, edges)
     return out.reshape(bins, rows, cols)
 
 

time: 40.5 us -> 39.1 us (0.965)
  waiting for transfers between devices: 12 us -> 10.7 us
    ppermute x1, waiting for transfers between devices: 1.25 us -> 0.01 us  [local(): edges = lax.ppermute(edge, 'band', beside)]
    pallas_call x1 -> x2, Pallas kernels: 3.65 us -> 3.46 us  [the longest x1 2.13 us: local(): call(col_kernel, 6, out_shape=jax.ShapeDtypeStruct(grouped, F32), in_spec...]
  transfers between devices with their start and end apart: 6 -> 6, of which waited for: 3 -> 2; matrix products, arithmetic and copies ran while one was open for 0% -> 0% of each run, Pallas kernels for 36% -> 43%
where the time goes in v5:
time: 39.1 us; the launch traced here: 38.8 us
  Pallas kernels  20.7 us (53%)
  waiting for transfers between devices  10.7 us (27%)
  starting transfers between devices  7.11 us (18%)
    ppermute x2, waiting for transfers between devices, local(): swapped.append(lax.ppermute(part, 'wide', swap))  10.7 us
    pallas_call x1, Pallas kernels, local(): call(near_kernel, 8, out_shape=[full, half, full], in_specs=[SMEM, HBM, V...  5.17 us
    pallas_call x1, Pallas kernels, local(): call(own_kernel, 9, out_shape=pltpu.HBM(full.shape, F32), in_specs=[SMEM,...  4.21 us
    ppermute x2, starting transfers between devices, local(): lax.ppermute(part, 'wide', relay_pairs(wide, i < len(sizes) - 1))  3.93 us
    pallas_call x1, Pallas kernels, local(): call(functools.partial(row_kernel, wide - 1), 10, out_shape=[full, jax.Sh...  2.91 us
    ppermute x2, starting transfers between devices, local(): swapped.append(lax.ppermute(part, 'wide', swap))  2.63 us
    pallas_call x2, Pallas kernels, prepare(): call(functools.partial(prepare_kernel, start), 8, out_shape=[jax.ShapeDty...  2.37 us
    pallas_call x1, Pallas kernels, local(): call(col_kernel, 6, out_shape=jax.ShapeDtypeStruct(grouped, F32), in_spec...  2.13 us
  transfers between devices with their start and end apart: 6, of which 2 were waited for; matrix products, arithmetic and copies ran while one was open for 0% of the time, Pallas kernels for 43%

profile of v5, /device:TPU:0, one launch (start us, length us, event | category | flops | bytes accessed | tf_op | source)
XLA Modules:
  0.0 38.8 jit_solution(17098550770161336209)
XLA Ops:
  0.0 0.5 %collective-permute-start = (bf16[2,576,1152]{2,1,0:T(8,128)(2,1)}, bf16[2,576,1152]{2,1,0:T(8,128)(2,1)S(1)}, u32[]{:S(2)}, u32[]{:S(2)}) collective-permute-start(bf16[2,576,1152]{2,1,0:T(8,128)(2,1)} %mine.3), channel_id=1, source_target_pairs={{0,1},{1,0},{2,3},{3,2},{4,5},{5,4},{6,7},{7,6},{8,9},{9,8},{10,11... | collective-permute-start | bytes 7962632 | tf_op jit(solution)/shard_map/ppermute | solution.py:361
  0.5 1.2 %shard_map.56.refs_0_ = bf16[2,576,128]{2,1,0:T(8,128)(2,1)S(1)} custom-call(f32[2304,128]{1,0:T(8,128)} %bitcast.13), custom_call_target="tpu_custom_call" | custom-call | tf_op jit(solution)/shard_map/pallas_call | solution.py:365
  1.7 2.5 %collective-permute-start.1 = (bf16[2,576,128]{2,1,0:T(8,128)(2,1)S(1)}, bf16[2,576,128]{2,1,0:T(8,128)(2,1)}, u32[]{:S(2)}, u32[]{:S(2)}) collective-permute-start(bf16[2,576,128]{2,1,0:T(8,128)(2,1)S(1)} %shard_map.56.refs_0_), channel_id=1, source_target_pairs={{0,2},{2,0},{4,6},{6,4},{8,10},{10,8},{12,14},{14,12},{1,3},{3,1},... | collective-permute-start | bytes 884744 | tf_op jit(solution)/shard_map/ppermute | solution.py:375
  4.2 1.2 %shard_map.57.refs_1_ = bf16[2,576,128]{2,1,0:T(8,128)(2,1)S(1)} custom-call(f32[2304,128]{1,0:T(8,128)} %bitcast.14), custom_call_target="tpu_custom_call" | custom-call | tf_op jit(solution)/shard_map/pallas_call | solution.py:365
  5.4 0.1 collective-permute-start.2
  5.5 6.7 %collective-permute-done.1.refs_0_ = bf16[2,576,128]{2,1,0:T(8,128)(2,1)} collective-permute-done((bf16[2,576,128]{2,1,0:T(8,128)(2,1)S(1)}, bf16[2,576,128]{2,1,0:T(8,128)(2,1)}, u32[]{:S(2)}, u32[]{:S(2)}) %collective-permute-start.1) | collective-permute-done | bytes 294944 | tf_op jit(solution)/shard_map/ppermute | solution.py:375
  12.2 2.1 %collective-permute-start.3 = (bf16[2,576,128]{2,1,0:T(8,128)(2,1)}, bf16[2,576,128]{2,1,0:T(8,128)(2,1)S(1)}, u32[]{:S(2)}, u32[]{:S(2)}) collective-permute-start(bf16[2,576,128]{2,1,0:T(8,128)(2,1)} %collective-permute-done.1.refs_0_), channel_id=1, source_target_pairs={{0,4},{4,8},{8,12},{12,0},{14,10},{10,6},{6,2},{2,14},{1,5},{5,9},... | collective-permute-start | bytes 884744 | tf_op jit(solution)/shard_map/ppermute | solution.py:377
  14.3 4.0 %collective-permute-done.2.refs_1_ = bf16[2,576,128]{2,1,0:T(8,128)(2,1)} collective-permute-done((bf16[2,576,128]{2,1,0:T(8,128)(2,1)S(1)}, bf16[2,576,128]{2,1,0:T(8,128)(2,1)}, u32[]{:S(2)}, u32[]{:S(2)}) %collective-permute-start.2) | collective-permute-done | bytes 294944 | tf_op jit(solution)/shard_map/ppermute | solution.py:375
  18.4 1.8 %collective-permute-start.4 = (bf16[2,576,128]{2,1,0:T(8,128)(2,1)}, bf16[2,576,128]{2,1,0:T(8,128)(2,1)}, u32[]{:S(2)}, u32[]{:S(2)}) collective-permute-start(bf16[2,576,128]{2,1,0:T(8,128)(2,1)} %collective-permute-done.2.refs_1_), channel_id=1, source_target_pairs={{0,4},{4,8},{8,12},{12,14},{14,10},{10,6},{6,2},{2,0},{1,5},{5,9},... | collective-permute-start | bytes 884744 | tf_op jit(solution)/shard_map/ppermute | solution.py:377
  20.2 0.0 copy-done.3
  20.2 1.5 %shard_map.55 = (f32[1152,128]{1,0:T(8,128)}, f32[1152,128]{1,0:T(8,128)}) custom-call(f32[9,128]{1,0:T(8,128)S(1)} %bitcast.11, s32[9,128]{1,0:T(8,128)S(1)} %bitcast.12), custom_call_target="tpu_custom_call" | custom-call | tf_op jit(solution)/shard_map/pallas_call | solution.py:395
  21.7 0.0 collective-permute-done.other
  21.7 4.2 %shard_map.58.own = f32[2,1152,128]{2,1,0:T(8,128)} custom-call(s32[1]{0:T(128)} %bitcast.band_ref, bf16[2,576,1152]{2,1,0:T(8,128)(2,1)} %mine.3, bf16[2,576,1152]{2,1,0:T(8,128)(2,1)S(1)} %collective-permute-done.other, f32[2304,128]{1,0:T(8,128)} %bitcast.15, bf16[2,576,128]{2,1,0:T(8,128)(2,1)S(1)} %shard_map.56.refs_0_, ...), custom_call_target="tpu_custom_call" | custom-call | tf_op jit(solution)/shard_map/pallas_call | solution.py:388
  25.9 5.2 %shard_map.59 = (f32[2,1152,128]{2,1,0:T(8,128)S(1)}, bf16[2,576,1152]{2,1,0:T(8,128)(2,1)S(1)}, f32[2,1152,128]{2,1,0:T(8,128)S(1)}) custom-call(s32[1]{0:T(128)} %bitcast.band_ref, bf16[2,576,1152]{2,1,0:T(8,128)(2,1)} %mine.3, bf16[2,576,1152]{2,1,0:T(8,128)(2,1)S(1)} %collective-permute-done.other, f32[2,1152,128]{2,1,0:T(8,128)} %shard_map.58.own, ...), custom_call_target="tpu_custom_call" | custom-call | tf_op jit(solution)/shard_map/pallas_call | solution.py:400
  31.1 0.0 collective-permute-done.3.refs_0_
  31.1 0.0 copy-start.1
  31.1 1.1 %shard_map.60.sums = f32[2,1152,256]{2,1,0:T(8,128)S(1)} custom-call(s32[1]{0:T(128)} %bitcast.band_ref, s32[1]{0:T(128)} %bitcast.1.wide_ref, bf16[2,576,1152]{2,1,0:T(8,128)(2,1)S(1)} %get-tuple-element.13.mine, bf16[2,576,1152]{2,1,0:T(8,128)(2,1)S(1)} %collective-permute-done.other, bf16[2,576,128]{2,1,0:T(8,128)(2,1)S(1)} %collective-permute-done.3.refs_0_), custom_call_target="tpu_custom_call" | custom-call | tf_op jit(solution)/shard_map/pallas_call | solution.py:406
  32.2 0.0 collective-permute-done.4.refs_1_
  32.3 0.0 copy-start.2
  32.3 2.9 %shard_map.61 = (f32[2,1152,128]{2,1,0:T(8,128)S(1)}, f32[144,128]{1,0:T(8,128)S(1)}) custom-call(s32[1]{0:T(128)} %bitcast.band_ref, s32[1]{0:T(128)} %bitcast.1.wide_ref, bf16[2,576,1152]{2,1,0:T(8,128)(2,1)S(1)} %get-tuple-element.13.mine, bf16[2,576,1152]{2,1,0:T(8,128)(2,1)S(1)} %collective-permute-done.other, f32[2,1152,256]{2,1,0:T(8,128)S(1)} %shard_map.60.sums, ...), custom_call_target="tpu_custom_call" | custom-call | tf_op jit(solution)/shard_map/pallas_call | solution.py:412
  35.2 0.1 collective-permute-start.5
  35.3 2.1 %shard_map.62.swept = f32[2,8,144,128]{3,2,1,0:T(8,128)S(1)} custom-call(s32[1]{0:T(128)} %bitcast.1.wide_ref, f32[8,144,128]{2,1,0:T(8,128)S(1)} %bitcast.8, s32[16,128]{1,0:T(8,128)S(1)} %copy-done.2, f32[2,8,144,128]{3,2,1,0:T(8,128)S(1)} %bitcast.10), custom_call_target="tpu_custom_call" | custom-call | tf_op jit(solution)/shard_map/pallas_call | solution.py:421
  37.4 0.0 collective-permute-done.5.beside
  37.4 1.3 %shard_map.63 = f32[2304,128]{1,0:T(8,128)} custom-call(s32[1]{0:T(128)} %bitcast.band_ref, s32[1]{0:T(128)} %bitcast.1.wide_ref, f32[8,144,128]{2,1,0:T(8,128)S(1)} %bitcast.9, s32[16,128]{1,0:T(8,128)S(1)} %copy-done.2, f32[2,8,144,128]{3,2,1,0:T(8,128)S(1)} %shard_map.62.swept, f32[144,128]{1,0:T(8,128)S(1)} %get-tuple-element.18.edge, ...), custom_call_target="tpu_custom_call" | custom-call | tf_op jit(solution)/shard_map/pallas_call | solution.py:425
  (7 shorter events, 0.0 us)
Async XLA Ops:
  0.0 21.7 %collective-permute-start = (bf16[2,576,1152]{2,1,0:T(8,128)(2,1)}, bf16[2,576,1152]{2,1,0:T(8,128)(2,1)S(1)}, u32[]{:S(2)}, u32[]{:S(2)}) collective-permute-start(bf16[2,576,1152]{2,1,0:T(8,128)(2,1)} %mine.3), channel_id=1, source_target_pairs={{0,1},{1,0},{2,3},{3,2},{4,5},{5,4},{6,7},{7,6},{8,9},{9,8},{10,11... | collective-permute-start | bytes 7962632 | tf_op jit(solution)/shard_map/ppermute | solution.py:361
  0.5 19.7 %copy-start.3 = (f32[1152]{0:T(1024)S(1)}, f32[1152]{0:T(1024)}, u32[]{:S(2)}) copy-start(f32[1152]{0:T(1024)} %param.7) | copy-start | bytes 13828
  0.5 19.7 %copy-start.4 = (s32[1152]{0:T(1024)S(1)}, s32[1152]{0:T(1024)}, u32[]{:S(2)}) copy-start(s32[1152]{0:T(1024)} %param.8) | copy-start | bytes 13828
  1.7 10.5 %collective-permute-start.1 = (bf16[2,576,128]{2,1,0:T(8,128)(2,1)S(1)}, bf16[2,576,128]{2,1,0:T(8,128)(2,1)}, u32[]{:S(2)}, u32[]{:S(2)}) collective-permute-start(bf16[2,576,128]{2,1,0:T(8,128)(2,1)S(1)} %shard_map.56.refs_0_), channel_id=1, source_target_pairs={{0,2},{2,0},{4,6},{6,4},{8,10},{10,8},{12,14},{14,12},{1,3},{3,1},... | collective-permute-start | bytes 884744 | tf_op jit(solution)/shard_map/ppermute | solution.py:375
  5.4 12.9 %collective-permute-start.2 = (bf16[2,576,128]{2,1,0:T(8,128)(2,1)S(1)}, bf16[2,576,128]{2,1,0:T(8,128)(2,1)}, u32[]{:S(2)}, u32[]{:S(2)}) collective-permute-start(bf16[2,576,128]{2,1,0:T(8,128)(2,1)S(1)} %shard_map.57.refs_1_), channel_id=1, source_target_pairs={{0,2},{2,0},{4,6},{6,4},{8,10},{10,8},{12,14},{14,12},{1,3},{3,1},... | collective-permute-start | bytes 884744 | tf_op jit(solution)/shard_map/ppermute | solution.py:375
  12.2 18.9 %collective-permute-start.3 = (bf16[2,576,128]{2,1,0:T(8,128)(2,1)}, bf16[2,576,128]{2,1,0:T(8,128)(2,1)S(1)}, u32[]{:S(2)}, u32[]{:S(2)}) collective-permute-start(bf16[2,576,128]{2,1,0:T(8,128)(2,1)} %collective-permute-done.1.refs_0_), channel_id=1, source_target_pairs={{0,4},{4,8},{8,12},{12,0},{14,10},{10,6},{6,2},{2,14},{1,5},{5,9},... | collective-permute-start | bytes 884744 | tf_op jit(solution)/shard_map/ppermute | solution.py:377
  18.4 13.9 %collective-permute-start.4 = (bf16[2,576,128]{2,1,0:T(8,128)(2,1)}, bf16[2,576,128]{2,1,0:T(8,128)(2,1)}, u32[]{:S(2)}, u32[]{:S(2)}) collective-permute-start(bf16[2,576,128]{2,1,0:T(8,128)(2,1)} %collective-permute-done.2.refs_1_), channel_id=1, source_target_pairs={{0,4},{4,8},{8,12},{12,14},{14,10},{10,6},{6,2},{2,0},{1,5},{5,9},... | collective-permute-start | bytes 884744 | tf_op jit(solution)/shard_map/ppermute | solution.py:377
  31.1 1.1 %copy-start.1 = (f32[1152,128]{1,0:T(8,128)S(1)}, f32[1152,128]{1,0:T(8,128)}, u32[]{:S(2)}) copy-start(f32[1152,128]{1,0:T(8,128)} %get-tuple-element.14.courants) | copy-start | bytes 1769476
  32.3 3.0 %copy-start = (f32[1152,128]{1,0:T(8,128)S(1)}, f32[1152,128]{1,0:T(8,128)}, u32[]{:S(2)}) copy-start(f32[1152,128]{1,0:T(8,128)} %get-tuple-element.12) | copy-start | bytes 1769476
  32.3 3.0 %copy-start.2 = (s32[16,128]{1,0:T(8,128)S(1)}, s32[16,128]{1,0:T(8,128)}, u32[]{:S(2)}) copy-start(s32[16,128]{1,0:T(8,128)} %sea.3) | copy-start | bytes 24580
  35.2 2.2 %collective-permute-start.5 = (f32[144,128]{1,0:T(8,128)S(1)}, f32[144,128]{1,0:T(8,128)S(1)}, u32[]{:S(2)}, u32[]{:S(2)}) collective-permute-start(f32[144,128]{1,0:T(8,128)S(1)} %get-tuple-element.18.edge), channel_id=1, source_target_pairs={{0,1},{1,0},{2,3},{3,2},{4,5},{5,4},{6,7},{7,6},{8,9},{9,8},{10,11... | collective-permute-start | bytes 221192 | tf_op jit(solution)/shard_map/ppermute | solution.py:418
